TPU v7x, 32 devices: a whole 2x2x4 slice. The times are simulated.
32 devices in a mesh: tile: 16 (over z, y, core), inner: 2 (over x).
Axes of the slice: x: 2, y: 2, z: 4, core: 2. Of those that a mesh axis runs over, the one named last changes fastest.
Arguments:
- amplitudes: bfloat16 [512, 4096], P('tile', 'inner'), may hold values from -6 to 6
- left_factors: bfloat16 [1024, 4096], P('tile', 'inner'), may hold values from -0.1875 to 0.1875
- right_factors: bfloat16 [1024, 16384], P(None, 'tile'), may hold values from -0.1875 to 0.1875
- tile_pattern: int32 [8, 32], replicated, may hold values from 0 to 1, as said below
- occupied_shift: float32 [512], P('inner'), may hold values from 0.5 to 2
- virtual_shift: float32 [16384], P('tile'), may hold values from 0.5 to 5
Outputs:
- residual: float32 [512, 16384], P('inner', 'tile')
Inputs may be any that keep to these rules, and one draw needn't show every extreme that they name: `tile_pattern`: 1 where the tiles interact, 0 where their integrals are dropped.
All inputs are finite; a program needn't handle non-finite values.
Results may differ from a plain program's by a relative error of at most 0.0029.
Values may be sent and summed in bfloat16 or wider, within the bound.
No kernel may reach another device: no remote copies, remote signals or barrier semaphores. Data moves between devices by JAX's collectives and lax.ppermute only.
A program may use at most 64 MiB of HBM per device.

v0:
```python
import jax
import jax.numpy as jnp
from jax import lax
from jax.sharding import PartitionSpec as P

TILE = 512


def on_device(amplitudes, left_factors, right_factors, tile_pattern, occupied_shift, virtual_shift):
    inner_place = lax.axis_index("inner")
    tile_place = lax.axis_index("tile")
    block_width = amplitudes.shape[1]
    out_width = right_factors.shape[1]
    left_tiles = block_width // TILE
    right_tiles = out_width // TILE
    gathered_rows = lax.all_gather(amplitudes, "tile", axis=0, tiled=True)
    local_mask = lax.dynamic_slice(
        tile_pattern,
        (inner_place * left_tiles, tile_place * right_tiles),
        (left_tiles, right_tiles),
    )
    factor_block = lax.all_gather(left_factors, "tile", axis=0, tiled=True)
    integrals = lax.dot_general(
        factor_block, right_factors, (((0,), (0,)), ((), ())), preferred_element_type=jnp.float32
    )
    shaped = integrals.reshape(left_tiles, TILE, right_tiles, TILE) * local_mask[
        :, None, :, None
    ].astype(jnp.float32)
    integrals = shaped.reshape(block_width, out_width).astype(jnp.bfloat16)
    partial_sum = jnp.dot(gathered_rows, integrals, preferred_element_type=jnp.float32)
    summed = lax.psum_scatter(partial_sum, "inner", scatter_dimension=0, tiled=True)
    return summed / (occupied_shift[:, None] + virtual_shift[None, :])


def solution(mesh):
    placed = (P("tile", "inner"), P("tile", "inner"), P(None, "tile"), P(), P("inner"), P("tile"))
    return jax.shard_map(
        on_device, mesh=mesh, in_specs=placed, out_specs=P("inner", "tile"), check_vma=False
    )
```

profile of v0, /device:TPU:10, one launch (start us, length us, event | category | flops | bytes accessed | tf_op | source)
XLA Modules:
  0.0 155.7 jit_solution(14859672486208603666)
XLA Ops:
  6.5 0.0 copy-start
  6.5 0.0 all-gather.5.cloned.1.call-start
  6.5 0.7 all-gather.5.cloned.1.call-update
  7.3 0.0 all-gather.3.cloned.1.call-start
  7.3 0.7 all-gather.3.cloned.1.call-update
  8.0 0.0 reduce-scatter.2.cloned.1.call-start
  8.1 0.8 dynamic-slice_convert_fusion
  8.8 5.5 %mul.19 = f32[4,512,2,512]{3,2,1,0:T(2,128)} broadcast(f32[4,2]{1,0:T(4,128)S(1)} %dynamic-slice_convert_fusion), dimensions={0,2} | broadcast | bytes 8388640 | tf_op jit(solution)/shard_map/mul | solution.py:26
  14.3 8.7 %copy.8 = f32[256,8,2,512]{3,1,2,0:T(8,128)} copy(f32[256,8,2,512]{3,2,1,0:T(2,128)} %bitcast.8) | data formatting | bytes 16777216
  23.0 28.0 %all-gather.5.cloned.1.call-done = bf16[512,2048]{1,0:T(8,128)(2,1)} async-done(((bf16[32,2048]{1,0:T(8,128)(2,1)}), bf16[512,2048]{1,0:T(8,128)(2,1)}) %all-gather.5.cloned.1.call-update) | async-done | bytes 2097168 | tf_op jit(solution)/shard_map/all_gather | solution.py:16
  51.0 52.5 %all-gather.3.cloned.1.call-done = bf16[1024,2048]{1,0:T(8,128)(2,1)} async-done(((bf16[64,2048]{1,0:T(8,128)(2,1)}), bf16[1024,2048]{1,0:T(8,128)(2,1)}) %all-gather.3.cloned.1.call-update) | async-done | bytes 4194320 | tf_op jit(solution)/shard_map/all_gather | solution.py:22
  103.5 0.0 copy-done
  103.5 0.0 copy-start.1
  103.5 0.0 copy-start.2
  103.5 13.3 %convolution_bitcast_fusion = f32[512,1024]{0,1:T(8,128)} fusion(bf16[512,2048]{1,0:T(8,128)(2,1)} %all-gather.5.cloned.1.call-done, f32[2048,1024]{1,0:T(8,128)} %bitcast.9, bf16[1024,2048]{1,0:T(8,128)(2,1)} %all-gather.3.cloned.1.call-done, bf16[1024,1024]{1,0:T(8,128)(2,1)S(1)} %copy-done), kind=kOutput, calls=%fused_computation.1 | convolution fusion | flops 6446645248 | bytes 18874368 | tf_op jit(solution)/shard_map/dot_general | solution.py:30
  116.8 0.0 reduce-scatter.2.cloned.1.call-update
  116.8 29.6 %reduce-scatter.2.cloned.1.call-done = f32[256,1024]{0,1:T(8,128)} async-done(((f32[512,1024]{0,1:T(8,128)}), f32[256,1024]{0,1:T(8,128)}) %reduce-scatter.2.cloned.1.call-update) | async-done | bytes 1048592 | tf_op jit(solution)/shard_map/reduce_scatter | solution.py:31
  146.5 0.0 copy-done.1
  146.5 0.0 copy-done.2
  146.5 1.4 add_divide_fusion
  147.9 1.3 copy.7
Async XLA Ops:
  6.5 96.9 %copy-start = (bf16[1024,1024]{1,0:T(8,128)(2,1)S(1)}, bf16[1024,1024]{1,0:T(8,128)(2,1)}, u32[]{:S(2)}) copy-start(bf16[1024,1024]{1,0:T(8,128)(2,1)} %param.8) | copy-start | bytes 6291460
  6.5 44.4 %all-gather.5.cloned.1.call-start = ((), (), s32[]{:S(2)}) async-start(), calls=%async_computation.2 | async-start | bytes 2228224 | tf_op jit(solution)/shard_map/all_gather | solution.py:16
  7.3 96.2 %all-gather.3.cloned.1.call-start = ((), (), s32[]{:S(2)}) async-start(), calls=%async_computation.1 | async-start | bytes 4456448 | tf_op jit(solution)/shard_map/all_gather | solution.py:22
  8.0 138.4 %reduce-scatter.2.cloned.1.call-start = ((), (), s32[]{:S(2)}) async-start(), calls=%async_computation.3 | async-start | bytes 3145728 | tf_op jit(solution)/shard_map/reduce_scatter | solution.py:31
  103.5 43.0 %copy-start.1 = (f32[1024]{0:T(1024)S(1)}, f32[1024]{0:T(1024)}, u32[]{:S(2)}) copy-start(f32[1024]{0:T(1024)} %param.11) | copy-start | bytes 12292
  103.5 43.0 %copy-start.2 = (f32[256]{0:T(256)S(1)}, f32[256]{0:T(256)}, u32[]{:S(2)}) copy-start(f32[256]{0:T(256)} %param.10) | copy-start | bytes 3076
Sparse Core Ops, SparseCore 0:
  9.5 41.4 all-gather.4
  53.1 50.2 all-gather.2
  116.9 29.4 reduce-scatter.1
where the time goes:
time: 158 us; the launch traced here: 156 us
  waiting for transfers between devices  112 us (71%)
  local copies, waits for them, and re-layouts  15.5 us (10%)
  matrix products  13.3 us (8%)
  between operations  13.1 us (8%)
  other arithmetic  2.2 us (1%)
    all_gather x1, waiting for transfers between devices, on_device(): factor_block = lax.all_gather(left_factors, 'tile', axis=0, tiled=True)  52.5 us
    reduce_scatter x1, waiting for transfers between devices, on_device(): lax.psum_scatter(partial_sum, 'inner', scatter_dimension=0, tiled=True)  29.6 us
    all_gather x1, waiting for transfers between devices, on_device(): gathered_rows = lax.all_gather(amplitudes, 'tile', axis=0, tiled=True)  28 us
    dot_general x1, matrix products, on_device(): jnp.dot(gathered_rows, integrals, preferred_element_type=jnp.float32)  13.3 us
    unnamed x7, local copies, waits for them, and re-layouts  8.7 us
    mul x1, local copies, waits for them, and re-layouts, on_device(): integrals.reshape(left_tiles, TILE, right_tiles, TILE)  5.46 us
  transfers between devices with their start and end apart: 3, of which 3 were waited for; matrix products, arithmetic and copies ran while one was open for 10% of the time, Pallas kernels for 0%

commit v1 on v0

v1 whole, which is shorter than its diff:
```python
import functools

import jax
import jax.numpy as jnp
from jax import lax
from jax.experimental import pallas as pl
from jax.experimental.pallas import tpu as pltpu
from jax.sharding import PartitionSpec as P

TILE = 512
VMEM = pl.BlockSpec(memory_space=pltpu.VMEM)
SMEM = pl.BlockSpec(memory_space=pltpu.SMEM)


def products_kernel(z_size, inner_size, place, *refs):
    a_refs, l_refs = refs[:z_size], refs[z_size : z_size + 4]
    outs = refs[z_size + 4 : z_size + 4 + inner_size]
    a_all, l_all = refs[z_size + 4 + inner_size :]
    z, y, core, inner = place[0], place[1], place[2], place[3]
    row_block, width = a_refs[0].shape
    col_block = l_refs[0].shape[0]
    for q, ref in enumerate(a_refs):
        a_all[pl.ds(pl.multiple_of((z ^ q) * row_block, row_block), row_block), :] = ref[...].astype(a_all.dtype)
    for q, ref in enumerate(l_refs):
        where = ((y ^ (q // 2)) * 2 + (core ^ (q % 2))) * col_block
        l_all[pl.ds(pl.multiple_of(where, col_block), col_block), :] = ref[...]
    group = z_size // inner_size * row_block
    for p, out in enumerate(outs):
        start = pl.multiple_of((inner ^ p) * group, group)
        for c in range(width // TILE):
            cols = slice(c * TILE, (c + 1) * TILE)
            left = a_all[pl.ds(start, group), cols].astype(jnp.bfloat16)
            out[c] = lax.dot_general(
                left, l_all[:, cols], (((1,), (1,)), ((), ())), preferred_element_type=jnp.float32
            ).astype(out.dtype)


def totals_kernel(inner_size, chips, right_tiles, place, pattern, *refs):
    mine, other = refs[:inner_size], refs[inner_size : 2 * inner_size]
    outs = refs[2 * inner_size :]
    chip, core, inner = place[0], place[1], place[2]
    left_tiles, rows, _ = mine[0].shape
    for m in range(chips):
        first = ((chip ^ m) * 2 + core) * right_tiles
        for d in range(right_tiles):
            for rel, source in enumerate((mine, other)):
                total = None
                for p, ref in enumerate(source):
                    for c in range(left_tiles):
                        on = pattern[(inner ^ p) * left_tiles + c, first + d] != 0
                        term = jnp.where(on, 1.0, 0.0) * ref[c].astype(jnp.float32)
                        total = term if total is None else total + term
                outs[m][d, rel * rows : (rel + 1) * rows, :] = total.astype(jnp.bfloat16)


def residual_kernel(chips, z_groups, place, *refs):
    t_refs = refs[:chips]
    right, occupied, virtual, out = refs[chips:]
    z, y, core = place[0], place[1], place[2]
    right_tiles, rows, depth = t_refs[0].shape
    row_block = rows // (2 * z_groups)
    for d in range(right_tiles):
        cols = slice(d * TILE, (d + 1) * TILE)
        total = None
        for q in range(chips // 2):
            left = jnp.concatenate([t_refs[2 * q][d], t_refs[2 * q + 1][d]], axis=0)
            start = pl.multiple_of((z ^ q) * depth, depth)
            term = jnp.dot(left, right[pl.ds(start, depth), cols], preferred_element_type=jnp.float32)
            total = term if total is None else total + term
        for rel_y in range(2):
            for rel in range(2):
                for s in range(z_groups):
                    at = ((s * 2 + (y ^ rel_y)) * 2 + (core ^ rel)) * row_block
                    at = pl.multiple_of(at, row_block)
                    source = rel_y * rows + rel * z_groups * row_block + s * row_block
                    shift = occupied[pl.ds(at, row_block), :] + virtual[:, cols]
                    out[pl.ds(at, row_block), cols] = total[source : source + row_block, :] / shift


def solution(mesh):
    tiles, inner_size = mesh.shape["tile"], mesh.shape["inner"]
    z_size, chips = tiles // 4, tiles // 2
    params = pltpu.CompilerParams(vmem_limit_bytes=48 * 1024 * 1024)

    def swap(value, q, axis="tile", size=tiles):
        return lax.ppermute(value, axis, [(t, t ^ q) for t in range(size)])

    def on_device(amplitudes, left_factors, right_factors, tile_pattern, occupied_shift, virtual_shift):
        t = lax.axis_index("tile")
        inner = lax.axis_index("inner")
        z, y, core = t // 4, lax.rem(t // 2, 2), lax.rem(t, 2)
        row_block, width = amplitudes.shape
        col_block = left_factors.shape[0]
        out_width = right_factors.shape[1]
        left_tiles, right_tiles = width // TILE, out_width // TILE
        z_groups = z_size // inner_size
        rows, depth = z_groups * row_block, 4 * col_block

        by_y = swap(left_factors, 2)
        amps = [amplitudes] + [swap(amplitudes, 4 * q) for q in range(1, z_size)]
        by_core = swap(left_factors, 1)
        by_both = swap(by_y, 1)

        packed = jnp.bfloat16 if row_block % 16 == 0 else jnp.float32
        products = pl.pallas_call(
            functools.partial(products_kernel, z_size, inner_size),
            out_shape=[
                jax.ShapeDtypeStruct((left_tiles, rows, depth), jnp.float32 if p == 0 else jnp.bfloat16)
                for p in range(inner_size)
            ],
            in_specs=[SMEM] + [VMEM] * (z_size + 4),
            out_specs=[VMEM] * inner_size,
            scratch_shapes=[
                pltpu.VMEM((z_size * row_block, width), packed),
                pltpu.VMEM((depth, width), jnp.bfloat16),
            ],
            compiler_params=params,
            cost_estimate=pl.CostEstimate(
                flops=2 * z_size * row_block * width * depth, bytes_accessed=2 << 20, transcendentals=0
            ),
            name="products",
        )(jnp.stack([z, y, core, inner]).astype(jnp.int32), *amps, left_factors, by_core, by_y, by_both)

        mine = [products[0]] + [swap(products[p], p, "inner", inner_size) for p in range(1, inner_size)]
        other = [swap(part, 1) for part in mine]

        totals = pl.pallas_call(
            functools.partial(totals_kernel, inner_size, chips, right_tiles),
            out_shape=[jax.ShapeDtypeStruct((right_tiles, 2 * rows, depth), jnp.bfloat16)] * chips,
            in_specs=[SMEM, SMEM] + [VMEM] * (2 * inner_size),
            out_specs=[VMEM] * chips,
            compiler_params=params,
            cost_estimate=pl.CostEstimate(flops=1 << 24, bytes_accessed=2 << 20, transcendentals=0),
            name="totals",
        )(jnp.stack([t // 2, core, inner]).astype(jnp.int32), tile_pattern, *mine, *other)

        arrived = [totals[0]] + [swap(totals[m], 2 * m) for m in range(1, chips)]

        return pl.pallas_call(
            functools.partial(residual_kernel, chips, z_groups),
            out_shape=jax.ShapeDtypeStruct((occupied_shift.shape[0], out_width), jnp.float32),
            in_specs=[SMEM] + [VMEM] * (chips + 3),
            out_specs=VMEM,
            compiler_params=params,
            cost_estimate=pl.CostEstimate(
                flops=2 * occupied_shift.shape[0] * out_width * right_factors.shape[0],
                bytes_accessed=4 << 20,
                transcendentals=0,
            ),
            name="residual",
        )(
            jnp.stack([z, y, core]).astype(jnp.int32),
            *arrived,
            right_factors,
            occupied_shift.reshape(-1, 1),
            virtual_shift.reshape(1, -1),
        )

    placed = (P("tile", "inner"), P("tile", "inner"), P(None, "tile"), P(), P("inner"), P("tile"))
    return jax.shard_map(
        on_device, mesh=mesh, in_specs=placed, out_specs=P("inner", "tile"), check_vma=False
    )
```

time: 158 us -> 69.2 us (0.44); the launches traced: 156 us -> 69 us
  waiting for transfers between devices: 112 us -> 42.6 us
  starting transfers between devices: 0.08 us -> 15.8 us
  matrix products: 13.3 us -> 0 us
  between operations: 13.1 us -> 0.04 us
  local copies, waits for them, and re-layouts: 15.5 us -> 4.04 us
  Pallas kernels: 0 us -> 6.22 us
  other arithmetic: 2.2 us -> 0.23 us
    all_gather x2 -> x0, waiting for transfers between devices: 80.5 us -> none  [the longest x1 52.5 us: on_device(): factor_block = lax.all_gather(left_factors, 'tile', axis=0, tiled=True)]
    ppermute x0 -> x16, waiting for transfers between devices: none -> 42.6 us  [swap(): return lax.ppermute(value, axis, [(t, t ^ q) for t in range(size)])]
    reduce_scatter x1 -> x0, waiting for transfers between devices: 29.6 us -> none  [on_device(): lax.psum_scatter(partial_sum, 'inner', scatter_dimension=0, tiled=True)]
    ppermute x0 -> x16, starting transfers between devices: none -> 15.8 us  [swap(): return lax.ppermute(value, axis, [(t, t ^ q) for t in range(size)])]
    dot_general x1 -> x0, matrix products: 13.3 us -> none  [on_device(): jnp.dot(gathered_rows, integrals, preferred_element_type=jnp.float32)]
    pallas_call x0 -> x3, Pallas kernels: none -> 6.22 us  [the longest x1 2.63 us: on_device(): pl.pallas_call(functools.partial(totals_kernel, inner_size, chips, right_...]
    unnamed x7 -> x10, local copies, waits for them, and re-layouts: 8.7 us -> 3.23 us
    mul x1 -> x0, local copies, waits for them, and re-layouts: 5.46 us -> none  [on_device(): integrals.reshape(left_tiles, TILE, right_tiles, TILE)]
  transfers between devices with their start and end apart: 3 -> 16, of which waited for: 3 -> 11; matrix products, arithmetic and copies ran while one was open for 10% -> 1% of each run, Pallas kernels for 0% -> 0%
where the time goes in v1:
time: 69.2 us; the launch traced here: 69 us
  waiting for transfers between devices  42.6 us (62%)
  starting transfers between devices  15.8 us (23%)
  Pallas kernels  6.22 us (9%)
  local copies, waits for them, and re-layouts  4.04 us (6%)
    ppermute x16, waiting for transfers between devices, swap(): return lax.ppermute(value, axis, [(t, t ^ q) for t in range(size)])  42.6 us
    ppermute x16, starting transfers between devices, swap(): return lax.ppermute(value, axis, [(t, t ^ q) for t in range(size)])  15.8 us
    unnamed x10, local copies, waits for them, and re-layouts  3.23 us
    pallas_call x1, Pallas kernels, on_device(): pl.pallas_call(functools.partial(totals_kernel, inner_size, chips, right_...  2.63 us
    pallas_call x1, Pallas kernels, on_device(): pl.pallas_call(functools.partial(residual_kernel, chips, z_groups), out_s...  2.23 us
  transfers between devices with their start and end apart: 16, of which 11 were waited for; matrix products, arithmetic and copies ran while one was open for 1% of the time, Pallas kernels for 0%

profile of v1, /device:TPU:10, one launch (start us, length us, event | category | flops | bytes accessed | tf_op | source)
XLA Modules:
  0.0 69.0 jit_solution(6860334502736916284)
XLA Ops:
  0.0 0.0 copy-start
  0.0 1.5 %collective-permute-start.4 = (bf16[64,2048]{1,0:T(8,128)(2,1)}, bf16[64,2048]{1,0:T(8,128)(2,1)S(1)}, u32[]{:S(2)}, u32[]{:S(2)}) collective-permute-start(bf16[64,2048]{1,0:T(8,128)(2,1)} %refs_4_.1), channel_id=1, source_target_pairs={{0,4},{2,6},{4,0},{6,2},{8,12},{10,14},{12,8},{14,10},{16,20},{18,... | collective-permute-start | bytes 786440 | tf_op jit(solution)/shard_map/ppermute | solution.py:86
  1.5 0.0 collective-permute-start.3
  1.5 6.7 %collective-permute-done.4.refs_6_ = bf16[64,2048]{1,0:T(8,128)(2,1)S(1)} collective-permute-done((bf16[64,2048]{1,0:T(8,128)(2,1)}, bf16[64,2048]{1,0:T(8,128)(2,1)S(1)}, u32[]{:S(2)}, u32[]{:S(2)}) %collective-permute-start.4) | collective-permute-done | bytes 262176 | tf_op jit(solution)/shard_map/ppermute | solution.py:86
  8.3 0.0 collective-permute-start.5
  8.3 2.6 %collective-permute-start.1 = (bf16[32,2048]{1,0:T(8,128)(2,1)}, bf16[32,2048]{1,0:T(8,128)(2,1)S(1)}, u32[]{:S(2)}, u32[]{:S(2)}) collective-permute-start(bf16[32,2048]{1,0:T(8,128)(2,1)} %refs_0_.1), channel_id=1, source_target_pairs={{0,16},{2,18},{4,20},{6,22},{8,24},{10,26},{12,28},{14,30},{16,0},... | collective-permute-start | bytes 393224 | tf_op jit(solution)/shard_map/ppermute | solution.py:86
  10.9 0.4 collective-permute-start
  11.3 0.5 collective-permute-start.2
  11.8 0.1 pad_add_fusion.2.place
  11.8 5.7 %collective-permute-done.1.refs_2_ = bf16[32,2048]{1,0:T(8,128)(2,1)S(1)} collective-permute-done((bf16[32,2048]{1,0:T(8,128)(2,1)}, bf16[32,2048]{1,0:T(8,128)(2,1)S(1)}, u32[]{:S(2)}, u32[]{:S(2)}) %collective-permute-start.1) | collective-permute-done | bytes 131104 | tf_op jit(solution)/shard_map/ppermute | solution.py:86
  17.6 1.1 %collective-permute-done.refs_1_ = bf16[32,2048]{1,0:T(8,128)(2,1)S(1)} collective-permute-done((bf16[32,2048]{1,0:T(8,128)(2,1)}, bf16[32,2048]{1,0:T(8,128)(2,1)S(1)}, u32[]{:S(2)}, u32[]{:S(2)}) %collective-permute-start) | collective-permute-done | bytes 131104 | tf_op jit(solution)/shard_map/ppermute | solution.py:86
  18.7 4.2 %collective-permute-done.2.refs_3_ = bf16[32,2048]{1,0:T(8,128)(2,1)S(1)} collective-permute-done((bf16[32,2048]{1,0:T(8,128)(2,1)}, bf16[32,2048]{1,0:T(8,128)(2,1)S(1)}, u32[]{:S(2)}, u32[]{:S(2)}) %collective-permute-start.2) | collective-permute-done | bytes 131104 | tf_op jit(solution)/shard_map/ppermute | solution.py:86
  22.9 0.0 collective-permute-done.3.refs_5_
  22.9 0.0 collective-permute-done.5.refs_7_
  22.9 0.0 copy-start.1
  22.9 0.9 %copy-done.1 = bf16[64,2048]{1,0:T(8,128)(2,1)S(1)} copy-done((bf16[64,2048]{1,0:T(8,128)(2,1)S(1)}, bf16[64,2048]{1,0:T(8,128)(2,1)}, u32[]{:S(2)}) %copy-start.1) | copy-done | bytes 262168
  23.9 0.0 copy-start.2
  23.9 0.9 %copy-done.2 = bf16[32,2048]{1,0:T(8,128)(2,1)S(1)} copy-done((bf16[32,2048]{1,0:T(8,128)(2,1)S(1)}, bf16[32,2048]{1,0:T(8,128)(2,1)}, u32[]{:S(2)}) %copy-start.2) | copy-done | bytes 131096
  24.8 1.4 %products.1 = (f32[4,64,256]{2,1,0:T(8,128)S(1)}, bf16[4,64,256]{2,1,0:T(8,128)(2,1)S(1)}) custom-call(s32[4]{0:T(128)S(1)} %pad_add_fusion.2.place, bf16[32,2048]{1,0:T(8,128)(2,1)S(1)} %copy-done.2, bf16[32,2048]{1,0:T(8,128)(2,1)S(1)} %collective-permute-done.refs_1_, bf16[32,2048]{1,0:T(8,128)(2,1)S(1)} %collective-permute-done.1.refs_2_, ...), custom_call_target="tpu_custom_call" | custom-call | flops 134217728 | bytes 2097152 | tf_op jit(solution)/shard_map/products/pallas_call | solution.py:105
  26.1 0.6 collective-permute-start.6
  26.7 0.0 collective-permute-start.7
  26.7 4.9 %collective-permute-done.6.refs_1_ = bf16[4,64,256]{2,1,0:T(8,128)(2,1)S(1)} collective-permute-done((bf16[4,64,256]{2,1,0:T(8,128)(2,1)S(1)}, bf16[4,64,256]{2,1,0:T(8,128)(2,1)S(1)}, u32[]{:S(2)}, u32[]{:S(2)}) %collective-permute-start.6) | collective-permute-done | bytes 131104 | tf_op jit(solution)/shard_map/ppermute | solution.py:86
  31.7 0.0 collective-permute-start.8
  31.7 0.1 pad_add_fusion.1.place
  31.8 0.0 collective-permute-done.7.refs_2_
  31.8 1.3 %collective-permute-done.8.refs_3_ = bf16[4,64,256]{2,1,0:T(8,128)(2,1)S(1)} collective-permute-done((bf16[4,64,256]{2,1,0:T(8,128)(2,1)S(1)}, bf16[4,64,256]{2,1,0:T(8,128)(2,1)S(1)}, u32[]{:S(2)}, u32[]{:S(2)}) %collective-permute-start.8) | collective-permute-done | bytes 131104 | tf_op jit(solution)/shard_map/ppermute | solution.py:86
  33.0 0.0 copy-start.3
  33.0 0.7 copy-done.3
  33.7 2.6 %totals.1 = (bf16[2,128,256]{2,1,0:T(8,128)(2,1)S(1)}, bf16[2,128,256]{2,1,0:T(8,128)(2,1)S(1)}, bf16[2,128,256]{2,1,0:T(8,128)(2,1)S(1)}, bf16[2,128,256]{2,1,0...) custom-call(s32[3]{0:T(128)S(1)} %pad_add_fusion.1.place, ...), custom_call_target="tpu_custom_call" | custom-call | flops 16777216 | bytes 2097152 | tf_op jit(solution)/shard_map/totals/pallas_call | solution.py:127
  36.3 1.5 %collective-permute-start.9 = (bf16[2,128,256]{2,1,0:T(8,128)(2,1)S(1)}, bf16[2,128,256]{2,1,0:T(8,128)(2,1)S(1)}, u32[]{:S(2)}, u32[]{:S(2)}) collective-permute-start(bf16[2,128,256]{2,1,0:T(8,128)(2,1)S(1)} %get-tuple-element.18), channel_id=1, source_target_pairs={{0,4},{2,6},{4,0},{6,2},{8,12},{10,14},{12,8},{14,10},{16,20},{18,... | collective-permute-start | bytes 393224 | tf_op jit(solution)/shard_map/ppermute | solution.py:86
  37.9 0.0 collective-permute-start.10
  37.9 2.0 %collective-permute-start.11 = (bf16[2,128,256]{2,1,0:T(8,128)(2,1)}, bf16[2,128,256]{2,1,0:T(8,128)(2,1)S(1)}, u32[]{:S(2)}, u32[]{:S(2)}) collective-permute-start(bf16[2,128,256]{2,1,0:T(8,128)(2,1)} %get-tuple-element.20), channel_id=1, source_target_pairs={{0,12},{2,14},{4,8},{6,10},{8,4},{10,6},{12,0},{14,2},{16,28},{18,... | collective-permute-start | bytes 393224 | tf_op jit(solution)/shard_map/ppermute | solution.py:86
  39.8 1.9 %collective-permute-start.12 = (bf16[2,128,256]{2,1,0:T(8,128)(2,1)}, bf16[2,128,256]{2,1,0:T(8,128)(2,1)S(1)}, u32[]{:S(2)}, u32[]{:S(2)}) collective-permute-start(bf16[2,128,256]{2,1,0:T(8,128)(2,1)} %get-tuple-element.21), channel_id=1, source_target_pairs={{0,16},{2,18},{4,20},{6,22},{8,24},{10,26},{12,28},{14,30},{16,0},... | collective-permute-start | bytes 393224 | tf_op jit(solution)/shard_map/ppermute | solution.py:86
  41.7 2.0 %collective-permute-start.13 = (bf16[2,128,256]{2,1,0:T(8,128)(2,1)}, bf16[2,128,256]{2,1,0:T(8,128)(2,1)S(1)}, u32[]{:S(2)}, u32[]{:S(2)}) collective-permute-start(bf16[2,128,256]{2,1,0:T(8,128)(2,1)} %get-tuple-element.22), channel_id=1, source_target_pairs={{0,20},{2,22},{4,16},{6,18},{8,28},{10,30},{12,24},{14,26},{16,4},... | collective-permute-start | bytes 393224 | tf_op jit(solution)/shard_map/ppermute | solution.py:86
  43.7 0.0 collective-permute-done.9.refs_1_
  43.7 2.4 %collective-permute-start.14 = (bf16[2,128,256]{2,1,0:T(8,128)(2,1)S(1)}, bf16[2,128,256]{2,1,0:T(8,128)(2,1)S(1)}, u32[]{:S(2)}, u32[]{:S(2)}) collective-permute-start(bf16[2,128,256]{2,1,0:T(8,128)(2,1)S(1)} %get-tuple-element.23), channel_id=1, source_target_pairs={{0,24},{2,26},{4,28},{6,30},{8,16},{10,18},{12,20},{14,22},{16,8},... | collective-permute-start | bytes 393224 | tf_op jit(solution)/shard_map/ppermute | solution.py:86
  46.1 0.0 collective-permute-done.10.refs_2_
  46.1 0.5 collective-permute-start.15
  46.5 0.8 %copy.7.refs_9_ = f32[256,1]{1,0:T(8,128)S(1)} copy(f32[256,1]{0,1:T(1,128)} %bitcast.8) | data formatting | bytes 2048 | tf_op jit(solution)/shard_map/reshape | solution.py:155
  47.4 0.1 pad_add_fusion.place
  47.4 1.0 %collective-permute-done.11.refs_3_ = bf16[2,128,256]{2,1,0:T(8,128)(2,1)S(1)} collective-permute-done((bf16[2,128,256]{2,1,0:T(8,128)(2,1)}, bf16[2,128,256]{2,1,0:T(8,128)(2,1)S(1)}, u32[]{:S(2)}, u32[]{:S(2)}) %collective-permute-start.11) | collective-permute-done | bytes 131104 | tf_op jit(solution)/shard_map/ppermute | solution.py:86
  48.4 8.6 %collective-permute-done.12.refs_4_ = bf16[2,128,256]{2,1,0:T(8,128)(2,1)S(1)} collective-permute-done((bf16[2,128,256]{2,1,0:T(8,128)(2,1)}, bf16[2,128,256]{2,1,0:T(8,128)(2,1)S(1)}, u32[]{:S(2)}, u32[]{:S(2)}) %collective-permute-start.12) | collective-permute-done | bytes 131104 | tf_op jit(solution)/shard_map/ppermute | solution.py:86
  57.0 3.0 %collective-permute-done.13.refs_5_ = bf16[2,128,256]{2,1,0:T(8,128)(2,1)S(1)} collective-permute-done((bf16[2,128,256]{2,1,0:T(8,128)(2,1)}, bf16[2,128,256]{2,1,0:T(8,128)(2,1)S(1)}, u32[]{:S(2)}, u32[]{:S(2)}) %collective-permute-start.13) | collective-permute-done | bytes 131104 | tf_op jit(solution)/shard_map/ppermute | solution.py:86
  60.0 4.1 %collective-permute-done.14.refs_6_ = bf16[2,128,256]{2,1,0:T(8,128)(2,1)S(1)} collective-permute-done((bf16[2,128,256]{2,1,0:T(8,128)(2,1)S(1)}, bf16[2,128,256]{2,1,0:T(8,128)(2,1)S(1)}, u32[]{:S(2)}, u32[]{:S(2)}) %collective-permute-start.14) | collective-permute-done | bytes 131104 | tf_op jit(solution)/shard_map/ppermute | solution.py:86
  64.1 2.0 %collective-permute-done.15.refs_7_ = bf16[2,128,256]{2,1,0:T(8,128)(2,1)S(1)} collective-permute-done((bf16[2,128,256]{2,1,0:T(8,128)(2,1)S(1)}, bf16[2,128,256]{2,1,0:T(8,128)(2,1)S(1)}, u32[]{:S(2)}, u32[]{:S(2)}) %collective-permute-start.15) | collective-permute-done | bytes 131104 | tf_op jit(solution)/shard_map/ppermute | solution.py:86
  66.1 0.0 copy-done
  66.1 0.0 copy-start.4
  66.1 0.7 copy-done.4
  66.7 2.2 %residual.1 = f32[256,1024]{1,0:T(8,128)} custom-call(s32[3]{0:T(128)S(1)} %pad_add_fusion.place, bf16[2,128,256]{2,1,0:T(8,128)(2,1)S(1)} %get-tuple-element.17.refs_0_, bf16[2,128,256]{2,1,0:T(8,128)(2,1)S(1)} %collective-permute-done.9.refs_1_, bf16[2,128,256]{2,1,0:T(8,128)(2,1)S(1)} %collective-permute-done.10.refs_2_, ...), custom_call_target="tpu_custom_call" | custom-call | flops 536870912 | bytes 4194304 | tf_op jit(solution)/shard_map/residual/pallas_call | solution.py:139
Async XLA Ops:
  0.0 66.1 %copy-start = (bf16[1024,1024]{1,0:T(8,128)(2,1)S(1)}, bf16[1024,1024]{1,0:T(8,128)(2,1)}, u32[]{:S(2)}) copy-start(bf16[1024,1024]{1,0:T(8,128)(2,1)} %refs_8_.1) | copy-start | bytes 6291460
  0.0 8.3 %collective-permute-start.4 = (bf16[64,2048]{1,0:T(8,128)(2,1)}, bf16[64,2048]{1,0:T(8,128)(2,1)S(1)}, u32[]{:S(2)}, u32[]{:S(2)}) collective-permute-start(bf16[64,2048]{1,0:T(8,128)(2,1)} %refs_4_.1), channel_id=1, source_target_pairs={{0,4},{2,6},{4,0},{6,2},{8,12},{10,14},{12,8},{14,10},{16,20},{18,... | collective-permute-start | bytes 786440 | tf_op jit(solution)/shard_map/ppermute | solution.py:86
  1.5 21.4 %collective-permute-start.3 = (bf16[64,2048]{1,0:T(8,128)(2,1)}, bf16[64,2048]{1,0:T(8,128)(2,1)S(1)}, u32[]{:S(2)}, u32[]{:S(2)}) collective-permute-start(bf16[64,2048]{1,0:T(8,128)(2,1)} %refs_4_.1), channel_id=1, source_target_pairs={{0,2},{2,0},{4,6},{6,4},{8,10},{10,8},{12,14},{14,12},{16,18},{18,... | collective-permute-start | bytes 786440 | tf_op jit(solution)/shard_map/ppermute | solution.py:86
  8.3 14.7 %collective-permute-start.5 = (bf16[64,2048]{1,0:T(8,128)(2,1)S(1)}, bf16[64,2048]{1,0:T(8,128)(2,1)S(1)}, u32[]{:S(2)}, u32[]{:S(2)}) collective-permute-start(bf16[64,2048]{1,0:T(8,128)(2,1)S(1)} %collective-permute-done.4.refs_6_), channel_id=1, source_target_pairs={{0,2},{2,0},{4,6},{6,4},{8,10},{10,8},{12,14},{14,12},{16,18},{18,... | collective-permute-start | bytes 786440 | tf_op jit(solution)/shard_map/ppermute | solution.py:86
  8.3 9.3 %collective-permute-start.1 = (bf16[32,2048]{1,0:T(8,128)(2,1)}, bf16[32,2048]{1,0:T(8,128)(2,1)S(1)}, u32[]{:S(2)}, u32[]{:S(2)}) collective-permute-start(bf16[32,2048]{1,0:T(8,128)(2,1)} %refs_0_.1), channel_id=1, source_target_pairs={{0,16},{2,18},{4,20},{6,22},{8,24},{10,26},{12,28},{14,30},{16,0},... | collective-permute-start | bytes 393224 | tf_op jit(solution)/shard_map/ppermute | solution.py:86
  10.9 7.9 %collective-permute-start = (bf16[32,2048]{1,0:T(8,128)(2,1)}, bf16[32,2048]{1,0:T(8,128)(2,1)S(1)}, u32[]{:S(2)}, u32[]{:S(2)}) collective-permute-start(bf16[32,2048]{1,0:T(8,128)(2,1)} %refs_0_.1), channel_id=1, source_target_pairs={{0,8},{2,10},{4,12},{6,14},{8,0},{10,2},{12,4},{14,6},{16,24},{18,... | collective-permute-start | bytes 393224 | tf_op jit(solution)/shard_map/ppermute | solution.py:86
  11.3 11.6 %collective-permute-start.2 = (bf16[32,2048]{1,0:T(8,128)(2,1)}, bf16[32,2048]{1,0:T(8,128)(2,1)S(1)}, u32[]{:S(2)}, u32[]{:S(2)}) collective-permute-start(bf16[32,2048]{1,0:T(8,128)(2,1)} %refs_0_.1), channel_id=1, source_target_pairs={{0,24},{2,26},{4,28},{6,30},{8,16},{10,18},{12,20},{14,22},{16,8},... | collective-permute-start | bytes 393224 | tf_op jit(solution)/shard_map/ppermute | solution.py:86
  22.9 1.0 %copy-start.1 = (bf16[64,2048]{1,0:T(8,128)(2,1)S(1)}, bf16[64,2048]{1,0:T(8,128)(2,1)}, u32[]{:S(2)}) copy-start(bf16[64,2048]{1,0:T(8,128)(2,1)} %refs_4_.1) | copy-start | bytes 786436
  23.9 0.9 %copy-start.2 = (bf16[32,2048]{1,0:T(8,128)(2,1)S(1)}, bf16[32,2048]{1,0:T(8,128)(2,1)}, u32[]{:S(2)}) copy-start(bf16[32,2048]{1,0:T(8,128)(2,1)} %refs_0_.1) | copy-start | bytes 393220
  26.1 5.5 %collective-permute-start.6 = (bf16[4,64,256]{2,1,0:T(8,128)(2,1)S(1)}, bf16[4,64,256]{2,1,0:T(8,128)(2,1)S(1)}, u32[]{:S(2)}, u32[]{:S(2)}) collective-permute-start(bf16[4,64,256]{2,1,0:T(8,128)(2,1)S(1)} %get-tuple-element.16), channel_id=1, source_target_pairs={{0,1},{1,0},{2,3},{3,2},{4,5},{5,4},{6,7},{7,6},{8,9},{9,8},{10,11... | collective-permute-start | bytes 393224 | tf_op jit(solution)/shard_map/ppermute | solution.py:86
  26.7 5.0 %collective-permute-start.7 = (f32[4,64,256]{2,1,0:T(8,128)S(1)}, f32[4,64,256]{2,1,0:T(8,128)S(1)}, u32[]{:S(2)}, u32[]{:S(2)}) collective-permute-start(f32[4,64,256]{2,1,0:T(8,128)S(1)} %get-tuple-element.15.refs_0_), channel_id=1, source_target_pairs={{0,2},{2,0},{4,6},{6,4},{8,10},{10,8},{12,14},{14,12},{16,18},{18,... | collective-permute-start | bytes 786440 | tf_op jit(solution)/shard_map/ppermute | solution.py:86
  31.7 1.3 %collective-permute-start.8 = (bf16[4,64,256]{2,1,0:T(8,128)(2,1)S(1)}, bf16[4,64,256]{2,1,0:T(8,128)(2,1)S(1)}, u32[]{:S(2)}, u32[]{:S(2)}) collective-permute-start(bf16[4,64,256]{2,1,0:T(8,128)(2,1)S(1)} %collective-permute-done.6.refs_1_), channel_id=1, source_target_pairs={{0,2},{2,0},{4,6},{6,4},{8,10},{10,8},{12,14},{14,12},{16,18},{18,... | collective-permute-start | bytes 393224 | tf_op jit(solution)/shard_map/ppermute | solution.py:86
  33.0 0.7 copy-start.3
  36.3 7.4 %collective-permute-start.9 = (bf16[2,128,256]{2,1,0:T(8,128)(2,1)S(1)}, bf16[2,128,256]{2,1,0:T(8,128)(2,1)S(1)}, u32[]{:S(2)}, u32[]{:S(2)}) collective-permute-start(bf16[2,128,256]{2,1,0:T(8,128)(2,1)S(1)} %get-tuple-element.18), channel_id=1, source_target_pairs={{0,4},{2,6},{4,0},{6,2},{8,12},{10,14},{12,8},{14,10},{16,20},{18,... | collective-permute-start | bytes 393224 | tf_op jit(solution)/shard_map/ppermute | solution.py:86
  37.9 8.2 %collective-permute-start.10 = (bf16[2,128,256]{2,1,0:T(8,128)(2,1)S(1)}, bf16[2,128,256]{2,1,0:T(8,128)(2,1)S(1)}, u32[]{:S(2)}, u32[]{:S(2)}) collective-permute-start(bf16[2,128,256]{2,1,0:T(8,128)(2,1)S(1)} %get-tuple-element.19), channel_id=1, source_target_pairs={{0,8},{2,10},{4,12},{6,14},{8,0},{10,2},{12,4},{14,6},{16,24},{18,... | collective-permute-start | bytes 393224 | tf_op jit(solution)/shard_map/ppermute | solution.py:86
  37.9 10.5 %collective-permute-start.11 = (bf16[2,128,256]{2,1,0:T(8,128)(2,1)}, bf16[2,128,256]{2,1,0:T(8,128)(2,1)S(1)}, u32[]{:S(2)}, u32[]{:S(2)}) collective-permute-start(bf16[2,128,256]{2,1,0:T(8,128)(2,1)} %get-tuple-element.20), channel_id=1, source_target_pairs={{0,12},{2,14},{4,8},{6,10},{8,4},{10,6},{12,0},{14,2},{16,28},{18,... | collective-permute-start | bytes 393224 | tf_op jit(solution)/shard_map/ppermute | solution.py:86
  39.8 17.2 %collective-permute-start.12 = (bf16[2,128,256]{2,1,0:T(8,128)(2,1)}, bf16[2,128,256]{2,1,0:T(8,128)(2,1)S(1)}, u32[]{:S(2)}, u32[]{:S(2)}) collective-permute-start(bf16[2,128,256]{2,1,0:T(8,128)(2,1)} %get-tuple-element.21), channel_id=1, source_target_pairs={{0,16},{2,18},{4,20},{6,22},{8,24},{10,26},{12,28},{14,30},{16,0},... | collective-permute-start | bytes 393224 | tf_op jit(solution)/shard_map/ppermute | solution.py:86
  41.7 18.2 %collective-permute-start.13 = (bf16[2,128,256]{2,1,0:T(8,128)(2,1)}, bf16[2,128,256]{2,1,0:T(8,128)(2,1)S(1)}, u32[]{:S(2)}, u32[]{:S(2)}) collective-permute-start(bf16[2,128,256]{2,1,0:T(8,128)(2,1)} %get-tuple-element.22), channel_id=1, source_target_pairs={{0,20},{2,22},{4,16},{6,18},{8,28},{10,30},{12,24},{14,26},{16,4},... | collective-permute-start | bytes 393224 | tf_op jit(solution)/shard_map/ppermute | solution.py:86
  43.7 20.4 %collective-permute-start.14 = (bf16[2,128,256]{2,1,0:T(8,128)(2,1)S(1)}, bf16[2,128,256]{2,1,0:T(8,128)(2,1)S(1)}, u32[]{:S(2)}, u32[]{:S(2)}) collective-permute-start(bf16[2,128,256]{2,1,0:T(8,128)(2,1)S(1)} %get-tuple-element.23), channel_id=1, source_target_pairs={{0,24},{2,26},{4,28},{6,30},{8,16},{10,18},{12,20},{14,22},{16,8},... | collective-permute-start | bytes 393224 | tf_op jit(solution)/shard_map/ppermute | solution.py:86
  46.1 20.0 %collective-permute-start.15 = (bf16[2,128,256]{2,1,0:T(8,128)(2,1)S(1)}, bf16[2,128,256]{2,1,0:T(8,128)(2,1)S(1)}, u32[]{:S(2)}, u32[]{:S(2)}) collective-permute-start(bf16[2,128,256]{2,1,0:T(8,128)(2,1)S(1)} %get-tuple-element.24), channel_id=1, source_target_pairs={{0,28},{2,30},{4,24},{6,26},{8,20},{10,22},{12,16},{14,18},{16,12}... | collective-permute-start | bytes 393224 | tf_op jit(solution)/shard_map/ppermute | solution.py:86
  66.1 0.7 copy-start.4

commit v2 on v1

--- a/solution.py
+++ b/solution.py
@@ -7,9 +7,17 @@
 from jax.experimental.pallas import tpu as pltpu
 from jax.sharding import PartitionSpec as P
 
+
 TILE = 512
 VMEM = pl.BlockSpec(memory_space=pltpu.VMEM)
 SMEM = pl.BlockSpec(memory_space=pltpu.SMEM)
+ANY = pl.BlockSpec(memory_space=pl.ANY)
+
+
+def keep_kernel(*refs):
+    half = len(refs) // 2
+    for source, target in zip(refs[:half], refs[half:]):
+        target[...] = source[...]
 
 
 def products_kernel(z_size, inner_size, place, *refs):
@@ -35,10 +43,12 @@
             ).astype(out.dtype)
 
 
-def totals_kernel(inner_size, chips, right_tiles, place, pattern, *refs):
+def totals_kernel(inner_size, chips, right_tiles, place, *refs):
     mine, other = refs[:inner_size], refs[inner_size : 2 * inner_size]
     outs = refs[2 * inner_size :]
-    chip, core, inner = place[0], place[1], place[2]
+    z, y, core, inner = place[0], place[1], place[2], place[3]
+    chip = z * 2 + y
+    columns = chips * 2 * right_tiles
     left_tiles, rows, _ = mine[0].shape
     for m in range(chips):
         first = ((chip ^ m) * 2 + core) * right_tiles
@@ -47,7 +57,7 @@
                 total = None
                 for p, ref in enumerate(source):
                     for c in range(left_tiles):
-                        on = pattern[(inner ^ p) * left_tiles + c, first + d] != 0
+                        on = place[4 + ((inner ^ p) * left_tiles + c) * columns + first + d] != 0
                         term = jnp.where(on, 1.0, 0.0) * ref[c].astype(jnp.float32)
                         total = term if total is None else total + term
                 outs[m][d, rel * rows : (rel + 1) * rows, :] = total.astype(jnp.bfloat16)
@@ -55,7 +65,9 @@
 
 def residual_kernel(chips, z_groups, place, *refs):
     t_refs = refs[:chips]
-    right, occupied, virtual, out = refs[chips:]
+    right, occupied, virtual_hbm, out, virtual, sem = refs[chips:]
+    fetch = pltpu.make_async_copy(virtual_hbm, virtual, sem)
+    fetch.start()
     z, y, core = place[0], place[1], place[2]
     right_tiles, rows, depth = t_refs[0].shape
     row_block = rows // (2 * z_groups)
@@ -67,6 +79,8 @@
             start = pl.multiple_of((z ^ q) * depth, depth)
             term = jnp.dot(left, right[pl.ds(start, depth), cols], preferred_element_type=jnp.float32)
             total = term if total is None else total + term
+        if d == 0:
+            fetch.wait()
         for rel_y in range(2):
             for rel in range(2):
                 for s in range(z_groups):
@@ -80,7 +94,7 @@
 def solution(mesh):
     tiles, inner_size = mesh.shape["tile"], mesh.shape["inner"]
     z_size, chips = tiles // 4, tiles // 2
-    params = pltpu.CompilerParams(vmem_limit_bytes=48 * 1024 * 1024)
+    params = pltpu.CompilerParams(vmem_limit_bytes=20 * 1024 * 1024)
 
     def swap(value, q, axis="tile", size=tiles):
         return lax.ppermute(value, axis, [(t, t ^ q) for t in range(size)])
@@ -97,9 +111,20 @@
         rows, depth = z_groups * row_block, 4 * col_block
 
         by_y = swap(left_factors, 2)
-        amps = [amplitudes] + [swap(amplitudes, 4 * q) for q in range(1, z_size)]
         by_core = swap(left_factors, 1)
         by_both = swap(by_y, 1)
+        moved = {q: swap(amplitudes, 4 * q) for q in range(1, z_size)}
+        place = jnp.stack([z, y, core, inner]).astype(jnp.int32)
+        place = jnp.concatenate([place, (tile_pattern != 0).astype(jnp.int32).reshape(-1)])
+        kept = pl.pallas_call(
+            keep_kernel,
+            out_shape=[pltpu.VMEM(v.shape, v.dtype) for v in (amplitudes, left_factors)],
+            in_specs=[VMEM] * 2,
+            out_specs=[VMEM] * 2,
+            cost_estimate=pl.CostEstimate(flops=0, bytes_accessed=1 << 20, transcendentals=0),
+            name="keep",
+        )(amplitudes, left_factors)
+        amps = [kept[0]] + [moved[q] for q in range(1, z_size)]
 
         packed = jnp.bfloat16 if row_block % 16 == 0 else jnp.float32
         products = pl.pallas_call(
@@ -119,7 +144,7 @@
                 flops=2 * z_size * row_block * width * depth, bytes_accessed=2 << 20, transcendentals=0
             ),
             name="products",
-        )(jnp.stack([z, y, core, inner]).astype(jnp.int32), *amps, left_factors, by_core, by_y, by_both)
+        )(place, *amps, kept[1], by_core, by_y, by_both)
 
         mine = [products[0]] + [swap(products[p], p, "inner", inner_size) for p in range(1, inner_size)]
         other = [swap(part, 1) for part in mine]
@@ -127,20 +152,21 @@
         totals = pl.pallas_call(
             functools.partial(totals_kernel, inner_size, chips, right_tiles),
             out_shape=[jax.ShapeDtypeStruct((right_tiles, 2 * rows, depth), jnp.bfloat16)] * chips,
-            in_specs=[SMEM, SMEM] + [VMEM] * (2 * inner_size),
+            in_specs=[SMEM] + [VMEM] * (2 * inner_size),
             out_specs=[VMEM] * chips,
             compiler_params=params,
             cost_estimate=pl.CostEstimate(flops=1 << 24, bytes_accessed=2 << 20, transcendentals=0),
             name="totals",
-        )(jnp.stack([t // 2, core, inner]).astype(jnp.int32), tile_pattern, *mine, *other)
+        )(place, *mine, *other)
 
         arrived = [totals[0]] + [swap(totals[m], 2 * m) for m in range(1, chips)]
 
         return pl.pallas_call(
             functools.partial(residual_kernel, chips, z_groups),
             out_shape=jax.ShapeDtypeStruct((occupied_shift.shape[0], out_width), jnp.float32),
-            in_specs=[SMEM] + [VMEM] * (chips + 3),
+            in_specs=[SMEM] + [VMEM] * (chips + 2) + [ANY],
             out_specs=VMEM,
+            scratch_shapes=[pltpu.VMEM((1, out_width), jnp.float32), pltpu.SemaphoreType.DMA(())],
             compiler_params=params,
             cost_estimate=pl.CostEstimate(
                 flops=2 * occupied_shift.shape[0] * out_width * right_factors.shape[0],
@@ -149,7 +175,7 @@
             ),
             name="residual",
         )(
-            jnp.stack([z, y, core]).astype(jnp.int32),
+            place,
             *arrived,
             right_factors,
             occupied_shift.reshape(-1, 1),
@@ -157,6 +183,5 @@
         )
 
     placed = (P("tile", "inner"), P("tile", "inner"), P(None, "tile"), P(), P("inner"), P("tile"))
-    return jax.shard_map(
-        on_device, mesh=mesh, in_specs=placed, out_specs=P("inner", "tile"), check_vma=False
-    )
+
+    return jax.shard_map(on_device, mesh=mesh, in_specs=placed, out_specs=P("inner", "tile"), check_vma=False)

time: 69.2 us -> 67.5 us (0.975)
  local copies, waits for them, and re-layouts: 4.04 us -> 0.31 us
  Pallas kernels: 6.22 us -> 7.74 us
    unnamed x10 -> x6, local copies, waits for them, and re-layouts: 3.23 us -> 0.01 us
    pallas_call x0 -> x1, Pallas kernels: none -> 1.04 us  [on_device(): pl.pallas_call(keep_kernel, out_shape=[pltpu.VMEM(v.shape, v.dtype) for v...]
  transfers between devices with their start and end apart: 16 -> 16, of which waited for: 11 -> 12; matrix products, arithmetic and copies ran while one was open for 1% -> 1% of each run, Pallas kernels for 0% -> 2%
where the time goes in v2:
time: 67.5 us; the launch traced here: 67.3 us
  waiting for transfers between devices  42.6 us (63%)
  starting transfers between devices  15.9 us (24%)
  Pallas kernels  7.74 us (11%)
  other arithmetic  0.69 us (1%)
    ppermute x16, waiting for transfers between devices, swap(): return lax.ppermute(value, axis, [(t, t ^ q) for t in range(size)])  42.6 us
    ppermute x16, starting transfers between devices, swap(): return lax.ppermute(value, axis, [(t, t ^ q) for t in range(size)])  15.9 us
    pallas_call x1, Pallas kernels, on_device(): pl.pallas_call(functools.partial(totals_kernel, inner_size, chips, right_...  2.54 us
    pallas_call x1, Pallas kernels, on_device(): pl.pallas_call(functools.partial(residual_kernel, chips, z_groups), out_s...  2.43 us
    pallas_call x1, Pallas kernels, on_device(): pl.pallas_call(functools.partial(products_kernel, z_size, inner_size), ou...  1.73 us
  transfers between devices with their start and end apart: 16, of which 12 were waited for; matrix products, arithmetic and copies ran while one was open for 1% of the time, Pallas kernels for 2%

profile of v2, /device:TPU:10, one launch (start us, length us, event | category | flops | bytes accessed | tf_op | source)
XLA Modules:
  0.0 67.3 jit_solution(12378660806443910335)
XLA Ops:
  0.0 0.0 copy-start.2
  0.0 0.0 copy-start.1
  0.0 0.0 copy-start
  0.0 1.6 %collective-permute-start.4 = (bf16[64,2048]{1,0:T(8,128)(2,1)}, bf16[64,2048]{1,0:T(8,128)(2,1)S(1)}, u32[]{:S(2)}, u32[]{:S(2)}) collective-permute-start(bf16[64,2048]{1,0:T(8,128)(2,1)} %refs_1_.1), channel_id=1, source_target_pairs={{0,4},{2,6},{4,0},{6,2},{8,12},{10,14},{12,8},{14,10},{16,20},{18,... | collective-permute-start | bytes 786440 | tf_op jit(solution)/shard_map/ppermute | solution.py:100
  1.6 0.0 collective-permute-start.3
  1.6 6.7 %collective-permute-done.4.refs_6_ = bf16[64,2048]{1,0:T(8,128)(2,1)S(1)} collective-permute-done((bf16[64,2048]{1,0:T(8,128)(2,1)}, bf16[64,2048]{1,0:T(8,128)(2,1)S(1)}, u32[]{:S(2)}, u32[]{:S(2)}) %collective-permute-start.4) | collective-permute-done | bytes 262176 | tf_op jit(solution)/shard_map/ppermute | solution.py:100
  8.3 0.0 collective-permute-start.5
  8.3 0.5 collective-permute-start
  8.8 2.7 %collective-permute-start.2 = (bf16[32,2048]{1,0:T(8,128)(2,1)}, bf16[32,2048]{1,0:T(8,128)(2,1)S(1)}, u32[]{:S(2)}, u32[]{:S(2)}) collective-permute-start(bf16[32,2048]{1,0:T(8,128)(2,1)} %refs_0_.1), channel_id=1, source_target_pairs={{0,24},{2,26},{4,28},{6,30},{8,16},{10,18},{12,20},{14,22},{16,8},... | collective-permute-start | bytes 393224 | tf_op jit(solution)/shard_map/ppermute | solution.py:100
  11.5 1.2 %collective-permute-start.1 = (bf16[32,2048]{1,0:T(8,128)(2,1)}, bf16[32,2048]{1,0:T(8,128)(2,1)}, u32[]{:S(2)}, u32[]{:S(2)}) collective-permute-start(bf16[32,2048]{1,0:T(8,128)(2,1)} %refs_0_.1), channel_id=1, source_target_pairs={{0,16},{2,18},{4,20},{6,22},{8,24},{10,26},{12,28},{14,30},{16,0},... | collective-permute-start | bytes 393224 | tf_op jit(solution)/shard_map/ppermute | solution.py:100
  12.7 1.0 %keep.1 = (bf16[32,2048]{1,0:T(8,128)(2,1)S(1)}, bf16[64,2048]{1,0:T(8,128)(2,1)S(1)}) custom-call(bf16[32,2048]{1,0:T(8,128)(2,1)} %refs_0_.1, bf16[64,2048]{1,0:T(8,128)(2,1)} %refs_1_.1), custom_call_target="tpu_custom_call" | custom-call | bytes 1048576 | tf_op jit(solution)/shard_map/keep/pallas_call | solution.py:119
  13.8 0.7 %compare_convert_fusion = s32[8,32]{1,0:T(8,128)S(1)} fusion(s32[8,32]{1,0:T(8,128)} %param.9), kind=kLoop, calls=%fused_computation | loop fusion | flops 512 | bytes 2048 | tf_op jit(solution)/shard_map/reshape | solution.py:118
  14.5 0.1 reshape.17
  14.6 0.1 concatenate.3.place
  14.6 0.3 collective-permute-done.refs_1_
  14.9 6.8 %collective-permute-done.2.refs_3_ = bf16[32,2048]{1,0:T(8,128)(2,1)S(1)} collective-permute-done((bf16[32,2048]{1,0:T(8,128)(2,1)}, bf16[32,2048]{1,0:T(8,128)(2,1)S(1)}, u32[]{:S(2)}, u32[]{:S(2)}) %collective-permute-start.2) | collective-permute-done | bytes 131104 | tf_op jit(solution)/shard_map/ppermute | solution.py:100
  21.7 1.7 %collective-permute-done.1.refs_2_ = bf16[32,2048]{1,0:T(8,128)(2,1)} collective-permute-done((bf16[32,2048]{1,0:T(8,128)(2,1)}, bf16[32,2048]{1,0:T(8,128)(2,1)}, u32[]{:S(2)}, u32[]{:S(2)}) %collective-permute-start.1) | collective-permute-done | bytes 131104 | tf_op jit(solution)/shard_map/ppermute | solution.py:100
  23.4 0.0 collective-permute-done.3.refs_5_
  23.4 0.0 collective-permute-done.5.refs_7_
  23.4 1.7 %products.1 = (f32[4,64,256]{2,1,0:T(8,128)S(1)}, bf16[4,64,256]{2,1,0:T(8,128)(2,1)S(1)}) custom-call(s32[260]{0:T(512)S(1)} %concatenate.3.place, bf16[32,2048]{1,0:T(8,128)(2,1)S(1)} %get-tuple-element.17.refs_0_, bf16[32,2048]{1,0:T(8,128)(2,1)S(1)} %collective-permute-done.refs_1_, bf16[32,2048]{1,0:T(8,128)(2,1)} %collective-permute-done.1.refs_2_, ...), custom_call_target="tpu_custom_call" | custom-call | flops 134217728 | bytes 2097152 | tf_op jit(solution)/shard_map/products/pallas_call | solution.py:130
  25.1 0.6 collective-permute-start.6
  25.7 0.0 collective-permute-start.7
  25.7 4.4 %collective-permute-done.6.refs_1_ = bf16[4,64,256]{2,1,0:T(8,128)(2,1)S(1)} collective-permute-done((bf16[4,64,256]{2,1,0:T(8,128)(2,1)S(1)}, bf16[4,64,256]{2,1,0:T(8,128)(2,1)S(1)}, u32[]{:S(2)}, u32[]{:S(2)}) %collective-permute-start.6) | collective-permute-done | bytes 131104 | tf_op jit(solution)/shard_map/ppermute | solution.py:100
  30.2 0.0 collective-permute-start.8
  30.2 0.0 collective-permute-done.7.refs_2_
  30.2 1.3 %collective-permute-done.8.refs_3_ = bf16[4,64,256]{2,1,0:T(8,128)(2,1)S(1)} collective-permute-done((bf16[4,64,256]{2,1,0:T(8,128)(2,1)S(1)}, bf16[4,64,256]{2,1,0:T(8,128)(2,1)S(1)}, u32[]{:S(2)}, u32[]{:S(2)}) %collective-permute-start.8) | collective-permute-done | bytes 131104 | tf_op jit(solution)/shard_map/ppermute | solution.py:100
  31.5 2.5 %totals.1 = (bf16[2,128,256]{2,1,0:T(8,128)(2,1)S(1)}, bf16[2,128,256]{2,1,0:T(8,128)(2,1)S(1)}, bf16[2,128,256]{2,1,0:T(8,128)(2,1)S(1)}, bf16[2,128,256]{2,1,0...) custom-call(s32[260]{0:T(512)S(1)} %concatenate.3.place, ...), custom_call_target="tpu_custom_call" | custom-call | flops 16777216 | bytes 2097152 | tf_op jit(solution)/shard_map/totals/pallas_call | solution.py:152
  34.0 1.5 %collective-permute-start.9 = (bf16[2,128,256]{2,1,0:T(8,128)(2,1)S(1)}, bf16[2,128,256]{2,1,0:T(8,128)(2,1)S(1)}, u32[]{:S(2)}, u32[]{:S(2)}) collective-permute-start(bf16[2,128,256]{2,1,0:T(8,128)(2,1)S(1)} %get-tuple-element.22), channel_id=1, source_target_pairs={{0,4},{2,6},{4,0},{6,2},{8,12},{10,14},{12,8},{14,10},{16,20},{18,... | collective-permute-start | bytes 393224 | tf_op jit(solution)/shard_map/ppermute | solution.py:100
  35.6 2.3 %collective-permute-start.10 = (bf16[2,128,256]{2,1,0:T(8,128)(2,1)S(1)}, bf16[2,128,256]{2,1,0:T(8,128)(2,1)S(1)}, u32[]{:S(2)}, u32[]{:S(2)}) collective-permute-start(bf16[2,128,256]{2,1,0:T(8,128)(2,1)S(1)} %get-tuple-element.23), channel_id=1, source_target_pairs={{0,8},{2,10},{4,12},{6,14},{8,0},{10,2},{12,4},{14,6},{16,24},{18,... | collective-permute-start | bytes 393224 | tf_op jit(solution)/shard_map/ppermute | solution.py:100
  37.9 0.0 collective-permute-start.11
  37.9 3.0 %collective-permute-start.12 = (bf16[2,128,256]{2,1,0:T(8,128)(2,1)}, bf16[2,128,256]{2,1,0:T(8,128)(2,1)S(1)}, u32[]{:S(2)}, u32[]{:S(2)}) collective-permute-start(bf16[2,128,256]{2,1,0:T(8,128)(2,1)} %get-tuple-element.25), channel_id=1, source_target_pairs={{0,16},{2,18},{4,20},{6,22},{8,24},{10,26},{12,28},{14,30},{16,0},... | collective-permute-start | bytes 393224 | tf_op jit(solution)/shard_map/ppermute | solution.py:100
  40.9 1.0 %collective-permute-start.13 = (bf16[2,128,256]{2,1,0:T(8,128)(2,1)}, bf16[2,128,256]{2,1,0:T(8,128)(2,1)S(1)}, u32[]{:S(2)}, u32[]{:S(2)}) collective-permute-start(bf16[2,128,256]{2,1,0:T(8,128)(2,1)} %get-tuple-element.26), channel_id=1, source_target_pairs={{0,20},{2,22},{4,16},{6,18},{8,28},{10,30},{12,24},{14,26},{16,4},... | collective-permute-start | bytes 393224 | tf_op jit(solution)/shard_map/ppermute | solution.py:100
  41.9 0.0 collective-permute-done.9.refs_1_
  41.9 1.5 %collective-permute-start.14 = (bf16[2,128,256]{2,1,0:T(8,128)(2,1)S(1)}, bf16[2,128,256]{2,1,0:T(8,128)(2,1)S(1)}, u32[]{:S(2)}, u32[]{:S(2)}) collective-permute-start(bf16[2,128,256]{2,1,0:T(8,128)(2,1)S(1)} %get-tuple-element.27), channel_id=1, source_target_pairs={{0,24},{2,26},{4,28},{6,30},{8,16},{10,18},{12,20},{14,22},{16,8},... | collective-permute-start | bytes 393224 | tf_op jit(solution)/shard_map/ppermute | solution.py:100
  43.3 1.9 %collective-permute-done.10.refs_2_ = bf16[2,128,256]{2,1,0:T(8,128)(2,1)S(1)} collective-permute-done((bf16[2,128,256]{2,1,0:T(8,128)(2,1)S(1)}, bf16[2,128,256]{2,1,0:T(8,128)(2,1)S(1)}, u32[]{:S(2)}, u32[]{:S(2)}) %collective-permute-start.10) | collective-permute-done | bytes 131104 | tf_op jit(solution)/shard_map/ppermute | solution.py:100
  45.2 0.0 collective-permute-start.15
  45.2 0.0 copy-done.2
  45.2 0.1 copy.7.refs_9_
  45.3 2.0 %collective-permute-done.11.refs_3_ = bf16[2,128,256]{2,1,0:T(8,128)(2,1)S(1)} collective-permute-done((bf16[2,128,256]{2,1,0:T(8,128)(2,1)}, bf16[2,128,256]{2,1,0:T(8,128)(2,1)S(1)}, u32[]{:S(2)}, u32[]{:S(2)}) %collective-permute-start.11) | collective-permute-done | bytes 131104 | tf_op jit(solution)/shard_map/ppermute | solution.py:100
  47.3 9.0 %collective-permute-done.12.refs_4_ = bf16[2,128,256]{2,1,0:T(8,128)(2,1)S(1)} collective-permute-done((bf16[2,128,256]{2,1,0:T(8,128)(2,1)}, bf16[2,128,256]{2,1,0:T(8,128)(2,1)S(1)}, u32[]{:S(2)}, u32[]{:S(2)}) %collective-permute-start.12) | collective-permute-done | bytes 131104 | tf_op jit(solution)/shard_map/ppermute | solution.py:100
  56.4 2.8 %collective-permute-done.13.refs_5_ = bf16[2,128,256]{2,1,0:T(8,128)(2,1)S(1)} collective-permute-done((bf16[2,128,256]{2,1,0:T(8,128)(2,1)}, bf16[2,128,256]{2,1,0:T(8,128)(2,1)S(1)}, u32[]{:S(2)}, u32[]{:S(2)}) %collective-permute-start.13) | collective-permute-done | bytes 131104 | tf_op jit(solution)/shard_map/ppermute | solution.py:100
  59.2 3.2 %collective-permute-done.14.refs_6_ = bf16[2,128,256]{2,1,0:T(8,128)(2,1)S(1)} collective-permute-done((bf16[2,128,256]{2,1,0:T(8,128)(2,1)S(1)}, bf16[2,128,256]{2,1,0:T(8,128)(2,1)S(1)}, u32[]{:S(2)}, u32[]{:S(2)}) %collective-permute-start.14) | collective-permute-done | bytes 131104 | tf_op jit(solution)/shard_map/ppermute | solution.py:100
  62.4 2.5 %collective-permute-done.15.refs_7_ = bf16[2,128,256]{2,1,0:T(8,128)(2,1)S(1)} collective-permute-done((bf16[2,128,256]{2,1,0:T(8,128)(2,1)S(1)}, bf16[2,128,256]{2,1,0:T(8,128)(2,1)S(1)}, u32[]{:S(2)}, u32[]{:S(2)}) %collective-permute-start.15) | collective-permute-done | bytes 131104 | tf_op jit(solution)/shard_map/ppermute | solution.py:100
  64.9 0.0 copy-done.1
  64.9 0.0 copy-done
  64.9 2.4 %residual.1 = f32[256,1024]{1,0:T(8,128)} custom-call(s32[260]{0:T(512)S(1)} %concatenate.3.place, bf16[2,128,256]{2,1,0:T(8,128)(2,1)S(1)} %get-tuple-element.21.refs_0_, bf16[2,128,256]{2,1,0:T(8,128)(2,1)S(1)} %collective-permute-done.9.refs_1_, bf16[2,128,256]{2,1,0:T(8,128)(2,1)S(1)} %collective-permute-done.10.refs_2_, ...), custom_call_target="tpu_custom_call" | custom-call | flops 536870912 | bytes 4194304 | tf_op jit(solution)/shard_map/residual/pallas_call | solution.py:164
Async XLA Ops:
  0.0 45.2 %copy-start.2 = (f32[256]{0:T(256)S(1)}, f32[256]{0:T(256)}, u32[]{:S(2)}) copy-start(f32[256]{0:T(256)} %param.10) | copy-start | bytes 3076
  0.0 64.9 %copy-start.1 = (f32[1024]{0:T(1024)S(1)}, f32[1024]{0:T(1024)}, u32[]{:S(2)}) copy-start(f32[1024]{0:T(1024)} %param.11) | copy-start | bytes 12292
  0.0 64.9 %copy-start = (bf16[1024,1024]{1,0:T(8,128)(2,1)S(1)}, bf16[1024,1024]{1,0:T(8,128)(2,1)}, u32[]{:S(2)}) copy-start(bf16[1024,1024]{1,0:T(8,128)(2,1)} %refs_8_.1) | copy-start | bytes 6291460
  0.0 8.3 %collective-permute-start.4 = (bf16[64,2048]{1,0:T(8,128)(2,1)}, bf16[64,2048]{1,0:T(8,128)(2,1)S(1)}, u32[]{:S(2)}, u32[]{:S(2)}) collective-permute-start(bf16[64,2048]{1,0:T(8,128)(2,1)} %refs_1_.1), channel_id=1, source_target_pairs={{0,4},{2,6},{4,0},{6,2},{8,12},{10,14},{12,8},{14,10},{16,20},{18,... | collective-permute-start | bytes 786440 | tf_op jit(solution)/shard_map/ppermute | solution.py:100
  1.6 21.8 %collective-permute-start.3 = (bf16[64,2048]{1,0:T(8,128)(2,1)}, bf16[64,2048]{1,0:T(8,128)(2,1)S(1)}, u32[]{:S(2)}, u32[]{:S(2)}) collective-permute-start(bf16[64,2048]{1,0:T(8,128)(2,1)} %refs_1_.1), channel_id=1, source_target_pairs={{0,2},{2,0},{4,6},{6,4},{8,10},{10,8},{12,14},{14,12},{16,18},{18,... | collective-permute-start | bytes 786440 | tf_op jit(solution)/shard_map/ppermute | solution.py:100
  8.3 15.1 %collective-permute-start.5 = (bf16[64,2048]{1,0:T(8,128)(2,1)S(1)}, bf16[64,2048]{1,0:T(8,128)(2,1)S(1)}, u32[]{:S(2)}, u32[]{:S(2)}) collective-permute-start(bf16[64,2048]{1,0:T(8,128)(2,1)S(1)} %collective-permute-done.4.refs_6_), channel_id=1, source_target_pairs={{0,2},{2,0},{4,6},{6,4},{8,10},{10,8},{12,14},{14,12},{16,18},{18,... | collective-permute-start | bytes 786440 | tf_op jit(solution)/shard_map/ppermute | solution.py:100
  8.3 6.6 %collective-permute-start = (bf16[32,2048]{1,0:T(8,128)(2,1)}, bf16[32,2048]{1,0:T(8,128)(2,1)S(1)}, u32[]{:S(2)}, u32[]{:S(2)}) collective-permute-start(bf16[32,2048]{1,0:T(8,128)(2,1)} %refs_0_.1), channel_id=1, source_target_pairs={{0,8},{2,10},{4,12},{6,14},{8,0},{10,2},{12,4},{14,6},{16,24},{18,... | collective-permute-start | bytes 393224 | tf_op jit(solution)/shard_map/ppermute | solution.py:100
  8.8 12.9 %collective-permute-start.2 = (bf16[32,2048]{1,0:T(8,128)(2,1)}, bf16[32,2048]{1,0:T(8,128)(2,1)S(1)}, u32[]{:S(2)}, u32[]{:S(2)}) collective-permute-start(bf16[32,2048]{1,0:T(8,128)(2,1)} %refs_0_.1), channel_id=1, source_target_pairs={{0,24},{2,26},{4,28},{6,30},{8,16},{10,18},{12,20},{14,22},{16,8},... | collective-permute-start | bytes 393224 | tf_op jit(solution)/shard_map/ppermute | solution.py:100
  11.5 11.9 %collective-permute-start.1 = (bf16[32,2048]{1,0:T(8,128)(2,1)}, bf16[32,2048]{1,0:T(8,128)(2,1)}, u32[]{:S(2)}, u32[]{:S(2)}) collective-permute-start(bf16[32,2048]{1,0:T(8,128)(2,1)} %refs_0_.1), channel_id=1, source_target_pairs={{0,16},{2,18},{4,20},{6,22},{8,24},{10,26},{12,28},{14,30},{16,0},... | collective-permute-start | bytes 393224 | tf_op jit(solution)/shard_map/ppermute | solution.py:100
  25.1 5.0 %collective-permute-start.6 = (bf16[4,64,256]{2,1,0:T(8,128)(2,1)S(1)}, bf16[4,64,256]{2,1,0:T(8,128)(2,1)S(1)}, u32[]{:S(2)}, u32[]{:S(2)}) collective-permute-start(bf16[4,64,256]{2,1,0:T(8,128)(2,1)S(1)} %get-tuple-element.20), channel_id=1, source_target_pairs={{0,1},{1,0},{2,3},{3,2},{4,5},{5,4},{6,7},{7,6},{8,9},{9,8},{10,11... | collective-permute-start | bytes 393224 | tf_op jit(solution)/shard_map/ppermute | solution.py:100
  25.7 4.4 %collective-permute-start.7 = (f32[4,64,256]{2,1,0:T(8,128)S(1)}, f32[4,64,256]{2,1,0:T(8,128)S(1)}, u32[]{:S(2)}, u32[]{:S(2)}) collective-permute-start(f32[4,64,256]{2,1,0:T(8,128)S(1)} %get-tuple-element.19.refs_0_), channel_id=1, source_target_pairs={{0,2},{2,0},{4,6},{6,4},{8,10},{10,8},{12,14},{14,12},{16,18},{18,... | collective-permute-start | bytes 786440 | tf_op jit(solution)/shard_map/ppermute | solution.py:100
  30.2 1.3 %collective-permute-start.8 = (bf16[4,64,256]{2,1,0:T(8,128)(2,1)S(1)}, bf16[4,64,256]{2,1,0:T(8,128)(2,1)S(1)}, u32[]{:S(2)}, u32[]{:S(2)}) collective-permute-start(bf16[4,64,256]{2,1,0:T(8,128)(2,1)S(1)} %collective-permute-done.6.refs_1_), channel_id=1, source_target_pairs={{0,2},{2,0},{4,6},{6,4},{8,10},{10,8},{12,14},{14,12},{16,18},{18,... | collective-permute-start | bytes 393224 | tf_op jit(solution)/shard_map/ppermute | solution.py:100
  34.0 7.8 %collective-permute-start.9 = (bf16[2,128,256]{2,1,0:T(8,128)(2,1)S(1)}, bf16[2,128,256]{2,1,0:T(8,128)(2,1)S(1)}, u32[]{:S(2)}, u32[]{:S(2)}) collective-permute-start(bf16[2,128,256]{2,1,0:T(8,128)(2,1)S(1)} %get-tuple-element.22), channel_id=1, source_target_pairs={{0,4},{2,6},{4,0},{6,2},{8,12},{10,14},{12,8},{14,10},{16,20},{18,... | collective-permute-start | bytes 393224 | tf_op jit(solution)/shard_map/ppermute | solution.py:100
  35.6 9.6 %collective-permute-start.10 = (bf16[2,128,256]{2,1,0:T(8,128)(2,1)S(1)}, bf16[2,128,256]{2,1,0:T(8,128)(2,1)S(1)}, u32[]{:S(2)}, u32[]{:S(2)}) collective-permute-start(bf16[2,128,256]{2,1,0:T(8,128)(2,1)S(1)} %get-tuple-element.23), channel_id=1, source_target_pairs={{0,8},{2,10},{4,12},{6,14},{8,0},{10,2},{12,4},{14,6},{16,24},{18,... | collective-permute-start | bytes 393224 | tf_op jit(solution)/shard_map/ppermute | solution.py:100
  37.9 9.4 %collective-permute-start.11 = (bf16[2,128,256]{2,1,0:T(8,128)(2,1)}, bf16[2,128,256]{2,1,0:T(8,128)(2,1)S(1)}, u32[]{:S(2)}, u32[]{:S(2)}) collective-permute-start(bf16[2,128,256]{2,1,0:T(8,128)(2,1)} %get-tuple-element.24), channel_id=1, source_target_pairs={{0,12},{2,14},{4,8},{6,10},{8,4},{10,6},{12,0},{14,2},{16,28},{18,... | collective-permute-start | bytes 393224 | tf_op jit(solution)/shard_map/ppermute | solution.py:100
  37.9 18.5 %collective-permute-start.12 = (bf16[2,128,256]{2,1,0:T(8,128)(2,1)}, bf16[2,128,256]{2,1,0:T(8,128)(2,1)S(1)}, u32[]{:S(2)}, u32[]{:S(2)}) collective-permute-start(bf16[2,128,256]{2,1,0:T(8,128)(2,1)} %get-tuple-element.25), channel_id=1, source_target_pairs={{0,16},{2,18},{4,20},{6,22},{8,24},{10,26},{12,28},{14,30},{16,0},... | collective-permute-start | bytes 393224 | tf_op jit(solution)/shard_map/ppermute | solution.py:100
  40.9 18.2 %collective-permute-start.13 = (bf16[2,128,256]{2,1,0:T(8,128)(2,1)}, bf16[2,128,256]{2,1,0:T(8,128)(2,1)S(1)}, u32[]{:S(2)}, u32[]{:S(2)}) collective-permute-start(bf16[2,128,256]{2,1,0:T(8,128)(2,1)} %get-tuple-element.26), channel_id=1, source_target_pairs={{0,20},{2,22},{4,16},{6,18},{8,28},{10,30},{12,24},{14,26},{16,4},... | collective-permute-start | bytes 393224 | tf_op jit(solution)/shard_map/ppermute | solution.py:100
  41.9 20.5 %collective-permute-start.14 = (bf16[2,128,256]{2,1,0:T(8,128)(2,1)S(1)}, bf16[2,128,256]{2,1,0:T(8,128)(2,1)S(1)}, u32[]{:S(2)}, u32[]{:S(2)}) collective-permute-start(bf16[2,128,256]{2,1,0:T(8,128)(2,1)S(1)} %get-tuple-element.27), channel_id=1, source_target_pairs={{0,24},{2,26},{4,28},{6,30},{8,16},{10,18},{12,20},{14,22},{16,8},... | collective-permute-start | bytes 393224 | tf_op jit(solution)/shard_map/ppermute | solution.py:100
  45.2 19.7 %collective-permute-start.15 = (bf16[2,128,256]{2,1,0:T(8,128)(2,1)S(1)}, bf16[2,128,256]{2,1,0:T(8,128)(2,1)S(1)}, u32[]{:S(2)}, u32[]{:S(2)}) collective-permute-start(bf16[2,128,256]{2,1,0:T(8,128)(2,1)S(1)} %get-tuple-element.28), channel_id=1, source_target_pairs={{0,28},{2,30},{4,24},{6,26},{8,20},{10,22},{12,16},{14,18},{16,12}... | collective-permute-start | bytes 393224 | tf_op jit(solution)/shard_map/ppermute | solution.py:100

commit v3 on v0

v3 whole, which is shorter than its diff:
```python
import functools

import jax
import jax.numpy as jnp
from jax import lax
from jax.experimental import pallas as pl
from jax.experimental.pallas import tpu as pltpu
from jax.sharding import PartitionSpec as P


TILE = 512
VMEM = pl.BlockSpec(memory_space=pltpu.VMEM)
SMEM = pl.BlockSpec(memory_space=pltpu.SMEM)
ANY = pl.BlockSpec(memory_space=pl.ANY)
PARAMS = pltpu.CompilerParams(vmem_limit_bytes=20 * 1024 * 1024)


def cost(flops, moved):
    return pl.CostEstimate(flops=int(flops), bytes_accessed=int(moved), transcendentals=0)


def keep_kernel(*refs):
    half = len(refs) // 2
    for source, target in zip(refs[:half], refs[half:]):
        target[...] = source[...]


def multiply(parts, place, a_refs, l_all, outs, a_all, result):
    z, inner = place[0], place[3]
    rows, width = a_refs[0].shape
    for r, ref in enumerate(a_refs):
        a_all[r * rows : (r + 1) * rows, :] = ref[...].astype(a_all.dtype)
    for c in range(width // TILE):
        cols = slice(c * TILE, (c + 1) * TILE)
        result[...] = lax.dot_general(
            a_all[:, cols].astype(jnp.bfloat16),
            l_all[:, cols],
            (((1,), (1,)), ((), ())),
            preferred_element_type=jnp.float32,
        )
        for p, out in enumerate(outs):
            start = pl.multiple_of((inner ^ p ^ (z // parts)) * rows, rows)
            out[c] = result[pl.ds(start, rows), :].astype(out.dtype)


def first_products_kernel(inner_size, parts, place, *refs):
    a_refs, l_refs = refs[:inner_size], refs[inner_size : inner_size + 4]
    outs = refs[inner_size + 4 : 2 * inner_size + 4]
    l_all, a_all, result = refs[2 * inner_size + 4 :]
    y, core = place[1], place[2]
    block = l_refs[0].shape[0]
    for q, ref in enumerate(l_refs):
        where = ((y ^ (q // 2)) * 2 + (core ^ (q % 2))) * block
        l_all[pl.ds(pl.multiple_of(where, block), block), :] = ref[...]
    multiply(parts, place, a_refs, l_all, outs, a_all, result)


def next_products_kernel(inner_size, parts, place, *refs):
    a_refs, l_all = refs[:inner_size], refs[inner_size]
    outs = refs[inner_size + 1 : 2 * inner_size + 1]
    a_all, result = refs[2 * inner_size + 1 :]
    multiply(parts, place, a_refs, l_all, outs, a_all, result)


def totals_kernel(inner_size, parts, targets, columns, right_tiles, place, *refs):
    count = 2 * inner_size * parts
    sources, outs = refs[:count], refs[count:]
    z, y, core, inner = place[0], place[1], place[2], place[3]
    chip = z * 2 + y
    left_tiles, rows, _ = sources[0].shape
    for m, out in zip(targets, outs):
        first = ((chip ^ m) * 2 + core) * right_tiles
        for d in range(right_tiles):
            for s in range(parts):
                blocks = []
                for rel in range(2):
                    total = None
                    for p in range(inner_size):
                        ref = sources[(s * 2 + rel) * inner_size + p]
                        for c in range(left_tiles):
                            on = place[4 + ((inner ^ p) * left_tiles + c) * columns + first + d] != 0
                            term = jnp.where(on, 1.0, 0.0) * ref[c].astype(jnp.float32)
                            total = term if total is None else total + term
                    blocks.append(total)
                at = slice(s * 2 * rows, (s + 1) * 2 * rows)
                out[d, at, :] = jnp.concatenate(blocks, axis=0).astype(jnp.bfloat16)


def residual_kernel(chips, parts, rows, place, *refs):
    half = chips // 2
    near, far = refs[:half], refs[half : half + parts * half]
    right, occupied, virtual_hbm, out, virtual, sem = refs[half + parts * half :]
    fetch = pltpu.make_async_copy(virtual_hbm, virtual, sem)
    fetch.start()
    z, y, core = place[0], place[1], place[2]
    right_tiles, _, depth = near[0].shape
    low = lax.rem(z, parts)

    def block(m, s, d):
        if m < half:
            return near[m][d, s * 2 * rows : (s + 1) * 2 * rows, :]
        return far[s * half + m - half][d]

    for d in range(right_tiles):
        cols = slice(d * TILE, (d + 1) * TILE)
        total = None
        for q in range(half):
            pieces = [block(2 * q + rel_y, o ^ (q % parts), d) for o in range(parts) for rel_y in range(2)]
            start = pl.multiple_of((z ^ q) * depth, depth)
            term = jnp.dot(
                jnp.concatenate(pieces, axis=0),
                right[pl.ds(start, depth), cols],
                preferred_element_type=jnp.float32,
            )
            total = term if total is None else total + term
        if d == 0:
            fetch.wait()
        source = 0
        for o in range(parts):
            for rel_y in range(2):
                for rel in range(2):
                    at = (((low ^ o) * 2 + (y ^ rel_y)) * 2 + (core ^ rel)) * rows
                    at = pl.multiple_of(at, rows)
                    shift = occupied[pl.ds(at, rows), :] + virtual[:, cols]
                    out[pl.ds(at, rows), cols] = total[source : source + rows, :] / shift
                    source += rows


def solution(mesh):
    tiles, inner_size = mesh.shape["tile"], mesh.shape["inner"]
    z_size, chips = tiles // 4, tiles // 2
    parts, half = z_size // inner_size, chips // 2

    def swap(value, q, axis="tile", size=tiles):
        return lax.ppermute(value, axis, [(t, t ^ q) for t in range(size)])

    def call(kernel, operands, in_specs, out_shape, scratch=(), flops=0, moved=1 << 20):
        many = isinstance(out_shape, list)
        return pl.pallas_call(
            kernel,
            out_shape=out_shape,
            in_specs=in_specs,
            out_specs=[VMEM] * len(out_shape) if many else VMEM,
            scratch_shapes=list(scratch),
            compiler_params=PARAMS,
            cost_estimate=cost(flops, moved),
        )(*operands)

    def on_device(amplitudes, left_factors, right_factors, tile_pattern, occupied_shift, virtual_shift):
        t = lax.axis_index("tile")
        inner = lax.axis_index("inner")
        z, y, core = t // 4, lax.rem(t // 2, 2), lax.rem(t, 2)
        rows, width = amplitudes.shape
        block = left_factors.shape[0]
        out_width = right_factors.shape[1]
        left_tiles, right_tiles = width // TILE, out_width // TILE
        depth = 4 * block

        place = jnp.stack([z, y, core, inner]).astype(jnp.int32)
        place = jnp.concatenate([place, (tile_pattern != 0).astype(jnp.int32).reshape(-1)])
        kept = call(
            keep_kernel,
            (amplitudes, left_factors),
            [VMEM] * 2,
            [pltpu.VMEM(v.shape, v.dtype) for v in (amplitudes, left_factors)],
        )
        by_y = swap(left_factors, 2)
        lefts = [kept[1], swap(left_factors, 1), by_y, swap(by_y, 1)]
        amps = {q: swap(amplitudes, 4 * q) for q in range(1, z_size)}
        amps[0] = kept[0]

        packed = jnp.bfloat16 if rows % 16 == 0 else jnp.float32
        scratch = [
            pltpu.VMEM((inner_size * rows, width), packed),
            pltpu.VMEM((inner_size * rows, depth), jnp.float32),
        ]
        shapes = [
            jax.ShapeDtypeStruct((left_tiles, rows, depth), jnp.float32 if p == 0 else jnp.bfloat16)
            for p in range(inner_size)
        ]
        flops = 2 * inner_size * rows * width * depth
        sources = []
        for s in range(parts):
            blocks = [amps[r * parts + s] for r in range(inner_size)]
            if s == 0:
                *products, left_all = call(
                    functools.partial(first_products_kernel, inner_size, parts),
                    (place, *blocks, *lefts),
                    [SMEM] + [VMEM] * (inner_size + 4),
                    shapes + [pltpu.VMEM((depth, width), jnp.bfloat16)],
                    scratch,
                    flops,
                )
            else:
                products = call(
                    functools.partial(next_products_kernel, inner_size, parts),
                    (place, *blocks, left_all),
                    [SMEM] + [VMEM] * (inner_size + 1),
                    shapes,
                    scratch,
                    flops,
                )
            mine = [products[0]]
            mine += [swap(products[p], p, "inner", inner_size) for p in range(1, inner_size)]
            other = [swap(part, 1) for part in mine]
            sources.append(mine + other)

        def totals(chosen, targets):
            operands = [ref for s in chosen for ref in sources[s]]
            return call(
                functools.partial(
                    totals_kernel, inner_size, len(chosen), targets, tile_pattern.shape[1], right_tiles
                ),
                (place, *operands),
                [SMEM] + [VMEM] * len(operands),
                [jax.ShapeDtypeStruct((right_tiles, len(chosen) * 2 * rows, depth), jnp.bfloat16)] * len(targets),
            )

        far = []
        for s in range(parts):
            made = totals([s], range(half, chips))
            far += [swap(made[m - half], 2 * m) for m in range(half, chips)]
        made = totals(range(parts), range(half))
        near = [made[0]] + [swap(made[m], 2 * m) for m in range(1, half)]

        return call(
            functools.partial(residual_kernel, chips, parts, rows),
            (
                place,
                *near,
                *far,
                right_factors,
                occupied_shift.reshape(-1, 1),
                virtual_shift.reshape(1, -1),
            ),
            [SMEM] + [VMEM] * (half + parts * half + 2) + [ANY],
            jax.ShapeDtypeStruct((occupied_shift.shape[0], out_width), jnp.float32),
            [pltpu.VMEM((1, out_width), jnp.float32), pltpu.SemaphoreType.DMA(())],
            2 * occupied_shift.shape[0] * out_width * right_factors.shape[0],
            4 << 20,
        )


    placed = (P("tile", "inner"), P("tile", "inner"), P(None, "tile"), P(), P("inner"), P("tile"))
    return jax.shard_map(on_device, mesh=mesh, in_specs=placed, out_specs=P("inner", "tile"), check_vma=False)
```

time: 158 us -> 65.6 us (0.42)
  the two profiles are of different devices: /device:TPU:10 before, /device:TPU:0 now
where the time goes in v3:
time: 65.6 us; the launch traced here: 65.4 us
  starting transfers between devices  31.7 us (48%)
  waiting for transfers between devices  20.4 us (31%)
  Pallas kernels  8.78 us (13%)
  local copies, waits for them, and re-layouts  3.72 us (6%)
  other arithmetic  0.69 us (1%)
    ppermute x23, starting transfers between devices, swap(): return lax.ppermute(value, axis, [(t, t ^ q) for t in range(size)])  31.7 us
    ppermute x23, waiting for transfers between devices, swap(): return lax.ppermute(value, axis, [(t, t ^ q) for t in range(size)])  20.4 us
    pallas_call x7, Pallas kernels, call(): pl.pallas_call(kernel, out_shape=out_shape, in_specs=in_specs, out_specs=...  8.78 us
    unnamed x14, local copies, waits for them, and re-layouts  3.42 us
  transfers between devices with their start and end apart: 23, of which 11 were waited for; matrix products, arithmetic and copies ran while one was open for 2% of the time, Pallas kernels for 8%

profile of v3, /device:TPU:0, one launch (start us, length us, event | category | flops | bytes accessed | tf_op | source)
XLA Modules:
  0.0 65.4 jit_solution(15072688734742329587)
XLA Ops:
  0.0 3.0 %collective-permute-start.2 = (bf16[64,2048]{1,0:T(8,128)(2,1)}, bf16[64,2048]{1,0:T(8,128)(2,1)S(1)}, u32[]{:S(2)}, u32[]{:S(2)}) collective-permute-start(bf16[64,2048]{1,0:T(8,128)(2,1)} %refs_1_.1), channel_id=1, source_target_pairs={{0,4},{2,6},{4,0},{6,2},{8,12},{10,14},{12,8},{14,10},{16,20},{18,... | collective-permute-start | bytes 786440 | tf_op jit(solution)/shard_map/ppermute | solution.py:135
  3.0 0.0 collective-permute-start.1
  3.0 6.5 %collective-permute-done.2.refs_4_ = bf16[64,2048]{1,0:T(8,128)(2,1)S(1)} collective-permute-done((bf16[64,2048]{1,0:T(8,128)(2,1)}, bf16[64,2048]{1,0:T(8,128)(2,1)S(1)}, u32[]{:S(2)}, u32[]{:S(2)}) %collective-permute-start.2) | collective-permute-done | bytes 262176 | tf_op jit(solution)/shard_map/ppermute | solution.py:135
  9.5 0.0 collective-permute-start.3
  9.5 2.8 %collective-permute-start = (bf16[32,2048]{1,0:T(8,128)(2,1)}, bf16[32,2048]{1,0:T(8,128)(2,1)S(1)}, u32[]{:S(2)}, u32[]{:S(2)}) collective-permute-start(bf16[32,2048]{1,0:T(8,128)(2,1)} %refs_0_.1), channel_id=1, source_target_pairs={{0,16},{2,18},{4,20},{6,22},{8,24},{10,26},{12,28},{14,30},{16,0},... | collective-permute-start | bytes 393224 | tf_op jit(solution)/shard_map/ppermute | solution.py:135
  12.3 1.6 %collective-permute-start.7 = (bf16[32,2048]{1,0:T(8,128)(2,1)}, bf16[32,2048]{1,0:T(8,128)(2,1)S(1)}, u32[]{:S(2)}, u32[]{:S(2)}) collective-permute-start(bf16[32,2048]{1,0:T(8,128)(2,1)} %refs_0_.1), channel_id=1, source_target_pairs={{0,8},{2,10},{4,12},{6,14},{8,0},{10,2},{12,4},{14,6},{16,24},{18,... | collective-permute-start | bytes 393224 | tf_op jit(solution)/shard_map/ppermute | solution.py:135
  13.9 0.0 collective-permute-start.8
  13.9 0.9 %copy-done.1 = bf16[64,2048]{1,0:T(8,128)(2,1)S(1)} copy-done((bf16[64,2048]{1,0:T(8,128)(2,1)S(1)}, bf16[64,2048]{1,0:T(8,128)(2,1)}, u32[]{:S(2)}) %copy-start.1) | copy-done | bytes 262168
  14.9 0.9 %copy-done.2 = bf16[32,2048]{1,0:T(8,128)(2,1)S(1)} copy-done((bf16[32,2048]{1,0:T(8,128)(2,1)S(1)}, bf16[32,2048]{1,0:T(8,128)(2,1)}, u32[]{:S(2)}) %copy-start.2) | copy-done | bytes 131096
  15.8 0.0 copy-start.3
  15.8 0.6 copy-done.3
  16.4 0.7 %compare_convert_fusion = s32[8,32]{1,0:T(8,128)S(1)} fusion(s32[8,32]{1,0:T(8,128)} %param.9), kind=kLoop, calls=%fused_computation | loop fusion | flops 512 | bytes 2048 | tf_op jit(solution)/shard_map/reshape | solution.py:160
  17.1 0.1 reshape.17
  17.2 0.1 concatenate.3.place
  17.3 2.5 %collective-permute-done.refs_1_ = bf16[32,2048]{1,0:T(8,128)(2,1)S(1)} collective-permute-done((bf16[32,2048]{1,0:T(8,128)(2,1)}, bf16[32,2048]{1,0:T(8,128)(2,1)S(1)}, u32[]{:S(2)}, u32[]{:S(2)}) %collective-permute-start) | collective-permute-done | bytes 131104 | tf_op jit(solution)/shard_map/ppermute | solution.py:135
  19.8 0.0 collective-permute-done.1.refs_3_
  19.8 0.0 collective-permute-done.3.refs_5_
  19.8 0.9 %copy-done.4 = bf16[32,2048]{1,0:T(8,128)(2,1)S(1)} copy-done((bf16[32,2048]{1,0:T(8,128)(2,1)S(1)}, bf16[32,2048]{1,0:T(8,128)(2,1)}, u32[]{:S(2)}) %copy-start.4) | copy-done | bytes 131096
  20.7 1.1 %shard_map.65 = (f32[4,32,256]{2,1,0:T(8,128)S(1)}, bf16[4,32,256]{2,1,0:T(8,128)(2,1)S(1)}, bf16[256,2048]{1,0:T(8,128)(2,1)S(1)}) custom-call(s32[260]{0:T(512)S(1)} %concatenate.3.place, bf16[32,2048]{1,0:T(8,128)(2,1)S(1)} %copy-done.4, bf16[32,2048]{1,0:T(8,128)(2,1)S(1)} %collective-permute-done.refs_1_, ...), custom_call_target="tpu_custom_call" | custom-call | flops 67108864 | bytes 1048576 | tf_op jit(solution)/shard_map/pallas_call | solution.py:139
  21.8 0.0 collective-permute-done.7.refs_0_
  21.9 1.7 %collective-permute-done.8.refs_1_ = bf16[32,2048]{1,0:T(8,128)(2,1)S(1)} collective-permute-done((bf16[32,2048]{1,0:T(8,128)(2,1)}, bf16[32,2048]{1,0:T(8,128)(2,1)S(1)}, u32[]{:S(2)}, u32[]{:S(2)}) %collective-permute-start.8) | collective-permute-done | bytes 131104 | tf_op jit(solution)/shard_map/ppermute | solution.py:135
  23.5 1.0 %shard_map.66 = (f32[4,32,256]{2,1,0:T(8,128)S(1)}, bf16[4,32,256]{2,1,0:T(8,128)(2,1)S(1)}) custom-call(s32[260]{0:T(512)S(1)} %concatenate.3.place, bf16[32,2048]{1,0:T(8,128)(2,1)S(1)} %collective-permute-done.7.refs_0_, bf16[32,2048]{1,0:T(8,128)(2,1)S(1)} %collective-permute-done.8.refs_1_, bf16[256,2048]{1,0:T(8,128)(2,1)S(1)} %get-tuple-element.28.refs_2_), custom_call_target="tpu_custom_call" | custom-call | flops 67108864 | bytes 1048576 | tf_op jit(solution)/shard_map/pallas_call | solution.py:139
  24.6 1.6 %collective-permute-start.9 = (bf16[4,32,256]{2,1,0:T(8,128)(2,1)S(1)}, bf16[4,32,256]{2,1,0:T(8,128)(2,1)S(1)}, u32[]{:S(2)}, u32[]{:S(2)}) collective-permute-start(bf16[4,32,256]{2,1,0:T(8,128)(2,1)S(1)} %get-tuple-element.30), channel_id=1, source_target_pairs={{0,1},{1,0},{2,3},{3,2},{4,5},{5,4},{6,7},{7,6},{8,9},{9,8},{10,11... | collective-permute-start | bytes 196616 | tf_op jit(solution)/shard_map/ppermute | solution.py:135
  26.1 0.0 collective-permute-start.10
  26.1 0.5 collective-permute-start.4
  26.7 0.2 collective-permute-start.5
  26.9 2.0 %collective-permute-done.9.refs_5_.refs_1_ = bf16[4,32,256]{2,1,0:T(8,128)(2,1)S(1)} collective-permute-done((bf16[4,32,256]{2,1,0:T(8,128)(2,1)S(1)}, bf16[4,32,256]{2,1,0:T(8,128)(2,1)S(1)}, u32[]{:S(2)}, u32[]{:S(2)}) %collective-permute-start.9) | collective-permute-done | bytes 65568 | tf_op jit(solution)/shard_map/ppermute | solution.py:135
  28.9 0.0 collective-permute-start.11
  28.9 1.7 %collective-permute-done.4.refs_1_ = bf16[4,32,256]{2,1,0:T(8,128)(2,1)S(1)} collective-permute-done((bf16[4,32,256]{2,1,0:T(8,128)(2,1)S(1)}, bf16[4,32,256]{2,1,0:T(8,128)(2,1)S(1)}, u32[]{:S(2)}, u32[]{:S(2)}) %collective-permute-start.4) | collective-permute-done | bytes 65568 | tf_op jit(solution)/shard_map/ppermute | solution.py:135
  30.6 0.0 collective-permute-start.6
  30.6 0.0 collective-permute-done.11.refs_7_.refs_3_
  30.6 0.0 collective-permute-done.10.refs_6_.refs_2_
  30.6 0.9 %shard_map.69 = (bf16[2,64,256]{2,1,0:T(8,128)(2,1)S(1)}, bf16[2,64,256]{2,1,0:T(8,128)(2,1)S(1)}, bf16[2,64,256]{2,1,0:T(8,128)(2,1)S(1)}, bf16[2,64,256]{2,1,0:T(8,128)(2,1)S(1)}) custom-call(s32[260]{0:T(512)S(1)} %concatenate.3.place, f32[4,32,256]{2,1,0:T(8,128)S(1)} %get-tuple-element.29.refs_4_.refs_0_, ...), custom_call_target="tpu_custom_call" | custom-call | bytes 1048576 | tf_op jit(solution)/shard_map/pallas_call | solution.py:139
  31.6 4.3 %collective-permute-start.19 = (bf16[2,64,256]{2,1,0:T(8,128)(2,1)S(1)}, bf16[2,64,256]{2,1,0:T(8,128)(2,1)S(1)}, u32[]{:S(2)}, u32[]{:S(2)}) collective-permute-start(bf16[2,64,256]{2,1,0:T(8,128)(2,1)S(1)} %get-tuple-element.39), channel_id=1, source_target_pairs={{0,16},{2,18},{4,20},{6,22},{8,24},{10,26},{12,28},{14,30},{16,0},... | collective-permute-start | bytes 196616 | tf_op jit(solution)/shard_map/ppermute | solution.py:135
  35.9 1.0 %collective-permute-start.20 = (bf16[2,64,256]{2,1,0:T(8,128)(2,1)S(1)}, bf16[2,64,256]{2,1,0:T(8,128)(2,1)S(1)}, u32[]{:S(2)}, u32[]{:S(2)}) collective-permute-start(bf16[2,64,256]{2,1,0:T(8,128)(2,1)S(1)} %get-tuple-element.40), channel_id=1, source_target_pairs={{0,20},{2,22},{4,16},{6,18},{8,28},{10,30},{12,24},{14,26},{16,4},... | collective-permute-start | bytes 196616 | tf_op jit(solution)/shard_map/ppermute | solution.py:135
  36.9 1.1 %collective-permute-start.21 = (bf16[2,64,256]{2,1,0:T(8,128)(2,1)S(1)}, bf16[2,64,256]{2,1,0:T(8,128)(2,1)S(1)}, u32[]{:S(2)}, u32[]{:S(2)}) collective-permute-start(bf16[2,64,256]{2,1,0:T(8,128)(2,1)S(1)} %get-tuple-element.41), channel_id=1, source_target_pairs={{0,24},{2,26},{4,28},{6,30},{8,16},{10,18},{12,20},{14,22},{16,8},... | collective-permute-start | bytes 196616 | tf_op jit(solution)/shard_map/ppermute | solution.py:135
  38.0 0.0 collective-permute-done.6.refs_3_
  38.0 2.7 %collective-permute-start.22 = (bf16[2,64,256]{2,1,0:T(8,128)(2,1)S(1)}, bf16[2,64,256]{2,1,0:T(8,128)(2,1)S(1)}, u32[]{:S(2)}, u32[]{:S(2)}) collective-permute-start(bf16[2,64,256]{2,1,0:T(8,128)(2,1)S(1)} %get-tuple-element.42), channel_id=1, source_target_pairs={{0,28},{2,30},{4,24},{6,26},{8,20},{10,22},{12,16},{14,18},{16,12}... | collective-permute-start | bytes 196616 | tf_op jit(solution)/shard_map/ppermute | solution.py:135
  40.7 0.0 collective-permute-done.5.refs_2_
  40.7 1.5 %shard_map.68 = (bf16[2,64,256]{2,1,0:T(8,128)(2,1)S(1)}, bf16[2,64,256]{2,1,0:T(8,128)(2,1)S(1)}, bf16[2,64,256]{2,1,0:T(8,128)(2,1)}, bf16[2,64,256]{2,1,0:T(8,128)(2,1)}) custom-call(s32[260]{0:T(512)S(1)} %concatenate.3.place, f32[4,32,256]{2,1,0:T(8,128)S(1)} %get-tuple-element.26.refs_0_, bf16[4,32,256]{2,1,0:T(8,128)(2,1)S(1)} %collective-permute-done.4.refs_1_, ...), custom_call_target="tpu_custom_call" | custom-call | bytes 1048576 | tf_op jit(solution)/shard_map/pallas_call | solution.py:139
  42.1 1.0 %collective-permute-start.15 = (bf16[2,64,256]{2,1,0:T(8,128)(2,1)S(1)}, bf16[2,64,256]{2,1,0:T(8,128)(2,1)S(1)}, u32[]{:S(2)}, u32[]{:S(2)}) collective-permute-start(bf16[2,64,256]{2,1,0:T(8,128)(2,1)S(1)} %get-tuple-element.35), channel_id=1, source_target_pairs={{0,16},{2,18},{4,20},{6,22},{8,24},{10,26},{12,28},{14,30},{16,0},... | collective-permute-start | bytes 196616 | tf_op jit(solution)/shard_map/ppermute | solution.py:135
  43.2 1.8 %shard_map.67 = (bf16[2,128,256]{2,1,0:T(8,128)(2,1)S(1)}, bf16[2,128,256]{2,1,0:T(8,128)(2,1)}, bf16[2,128,256]{2,1,0:T(8,128)(2,1)S(1)}, bf16[2,128,256]{2,1,0:T(8,128)(2,1)S(1)}) custom-call(s32[260]{0:T(512)S(1)} %concatenate.3.place, f32[4,32,256]{2,1,0:T(8,128)S(1)} %get-tuple-element.26.refs_0_, ...), custom_call_target="tpu_custom_call" | custom-call | bytes 1048576 | tf_op jit(solution)/shard_map/pallas_call | solution.py:139
  45.0 0.1 collective-permute-done.19.refs_8_
  45.1 2.7 %collective-permute-start.16 = (bf16[2,64,256]{2,1,0:T(8,128)(2,1)S(1)}, bf16[2,64,256]{2,1,0:T(8,128)(2,1)S(1)}, u32[]{:S(2)}, u32[]{:S(2)}) collective-permute-start(bf16[2,64,256]{2,1,0:T(8,128)(2,1)S(1)} %get-tuple-element.36), channel_id=1, source_target_pairs={{0,20},{2,22},{4,16},{6,18},{8,28},{10,30},{12,24},{14,26},{16,4},... | collective-permute-start | bytes 196616 | tf_op jit(solution)/shard_map/ppermute | solution.py:135
  47.9 0.3 collective-permute-done.20.refs_9_
  48.2 0.5 collective-permute-start.12
  48.7 0.0 collective-permute-done.21.refs_10_
  48.7 0.5 collective-permute-start.13
  49.2 0.0 collective-permute-done.22.refs_11_
  49.2 3.7 %collective-permute-start.14 = (bf16[2,128,256]{2,1,0:T(8,128)(2,1)S(1)}, bf16[2,128,256]{2,1,0:T(8,128)(2,1)S(1)}, u32[]{:S(2)}, u32[]{:S(2)}) collective-permute-start(bf16[2,128,256]{2,1,0:T(8,128)(2,1)S(1)} %get-tuple-element.34), channel_id=1, source_target_pairs={{0,12},{2,14},{4,8},{6,10},{8,4},{10,6},{12,0},{14,2},{16,28},{18,... | collective-permute-start | bytes 393224 | tf_op jit(solution)/shard_map/ppermute | solution.py:135
  52.9 0.0 collective-permute-done.15.refs_4_
  53.0 1.9 %collective-permute-start.17 = (bf16[2,64,256]{2,1,0:T(8,128)(2,1)}, bf16[2,64,256]{2,1,0:T(8,128)(2,1)S(1)}, u32[]{:S(2)}, u32[]{:S(2)}) collective-permute-start(bf16[2,64,256]{2,1,0:T(8,128)(2,1)} %get-tuple-element.37), channel_id=1, source_target_pairs={{0,24},{2,26},{4,28},{6,30},{8,16},{10,18},{12,20},{14,22},{16,8},... | collective-permute-start | bytes 196616 | tf_op jit(solution)/shard_map/ppermute | solution.py:135
  54.9 0.4 collective-permute-done.16.refs_5_
  55.3 2.5 %collective-permute-start.18 = (bf16[2,64,256]{2,1,0:T(8,128)(2,1)}, bf16[2,64,256]{2,1,0:T(8,128)(2,1)S(1)}, u32[]{:S(2)}, u32[]{:S(2)}) collective-permute-start(bf16[2,64,256]{2,1,0:T(8,128)(2,1)} %get-tuple-element.38), channel_id=1, source_target_pairs={{0,28},{2,30},{4,24},{6,26},{8,20},{10,22},{12,16},{14,18},{16,12}... | collective-permute-start | bytes 196616 | tf_op jit(solution)/shard_map/ppermute | solution.py:135
  57.8 0.0 copy-done.6
  57.8 0.1 copy.7.refs_13_
  57.9 1.3 %collective-permute-done.17.refs_6_ = bf16[2,64,256]{2,1,0:T(8,128)(2,1)S(1)} collective-permute-done((bf16[2,64,256]{2,1,0:T(8,128)(2,1)}, bf16[2,64,256]{2,1,0:T(8,128)(2,1)S(1)}, u32[]{:S(2)}, u32[]{:S(2)}) %collective-permute-start.17) | collective-permute-done | bytes 65568 | tf_op jit(solution)/shard_map/ppermute | solution.py:135
  59.3 3.3 %collective-permute-done.18.refs_7_ = bf16[2,64,256]{2,1,0:T(8,128)(2,1)S(1)} collective-permute-done((bf16[2,64,256]{2,1,0:T(8,128)(2,1)}, bf16[2,64,256]{2,1,0:T(8,128)(2,1)S(1)}, u32[]{:S(2)}, u32[]{:S(2)}) %collective-permute-start.18) | collective-permute-done | bytes 65568 | tf_op jit(solution)/shard_map/ppermute | solution.py:135
  62.6 0.0 collective-permute-done.12.refs_1_
  62.6 0.0 collective-permute-done.13.refs_2_
  62.6 0.4 collective-permute-done.14.refs_3_
  62.9 0.0 copy-done
  62.9 0.0 copy-done.5
  62.9 2.4 %shard_map.70 = f32[256,1024]{1,0:T(8,128)} custom-call(s32[260]{0:T(512)S(1)} %concatenate.3.place, bf16[2,128,256]{2,1,0:T(8,128)(2,1)S(1)} %get-tuple-element.31.refs_0_, bf16[2,128,256]{2,1,0:T(8,128)(2,1)S(1)} %collective-permute-done.12.refs_1_, bf16[2,128,256]{2,1,0:T(8,128)(2,1)S(1)} %collective-permute-done.13.refs_2_, ...), custom_call_target="tpu_custom_call" | custom-call | flops 536870912 | bytes 4194304 | tf_op jit(solution)/shard_map/pallas_call | solution.py:139
  (7 shorter events, 0.0 us)
Async XLA Ops:
  0.0 9.5 %collective-permute-start.2 = (bf16[64,2048]{1,0:T(8,128)(2,1)}, bf16[64,2048]{1,0:T(8,128)(2,1)S(1)}, u32[]{:S(2)}, u32[]{:S(2)}) collective-permute-start(bf16[64,2048]{1,0:T(8,128)(2,1)} %refs_1_.1), channel_id=1, source_target_pairs={{0,4},{2,6},{4,0},{6,2},{8,12},{10,14},{12,8},{14,10},{16,20},{18,... | collective-permute-start | bytes 786440 | tf_op jit(solution)/shard_map/ppermute | solution.py:135
  3.0 16.8 %collective-permute-start.1 = (bf16[64,2048]{1,0:T(8,128)(2,1)}, bf16[64,2048]{1,0:T(8,128)(2,1)S(1)}, u32[]{:S(2)}, u32[]{:S(2)}) collective-permute-start(bf16[64,2048]{1,0:T(8,128)(2,1)} %refs_1_.1), channel_id=1, source_target_pairs={{0,2},{2,0},{4,6},{6,4},{8,10},{10,8},{12,14},{14,12},{16,18},{18,... | collective-permute-start | bytes 786440 | tf_op jit(solution)/shard_map/ppermute | solution.py:135
  9.5 10.3 %collective-permute-start.3 = (bf16[64,2048]{1,0:T(8,128)(2,1)S(1)}, bf16[64,2048]{1,0:T(8,128)(2,1)S(1)}, u32[]{:S(2)}, u32[]{:S(2)}) collective-permute-start(bf16[64,2048]{1,0:T(8,128)(2,1)S(1)} %collective-permute-done.2.refs_4_), channel_id=1, source_target_pairs={{0,2},{2,0},{4,6},{6,4},{8,10},{10,8},{12,14},{14,12},{16,18},{18,... | collective-permute-start | bytes 786440 | tf_op jit(solution)/shard_map/ppermute | solution.py:135
  9.5 10.3 %collective-permute-start = (bf16[32,2048]{1,0:T(8,128)(2,1)}, bf16[32,2048]{1,0:T(8,128)(2,1)S(1)}, u32[]{:S(2)}, u32[]{:S(2)}) collective-permute-start(bf16[32,2048]{1,0:T(8,128)(2,1)} %refs_0_.1), channel_id=1, source_target_pairs={{0,16},{2,18},{4,20},{6,22},{8,24},{10,26},{12,28},{14,30},{16,0},... | collective-permute-start | bytes 393224 | tf_op jit(solution)/shard_map/ppermute | solution.py:135
  12.3 9.5 %collective-permute-start.7 = (bf16[32,2048]{1,0:T(8,128)(2,1)}, bf16[32,2048]{1,0:T(8,128)(2,1)S(1)}, u32[]{:S(2)}, u32[]{:S(2)}) collective-permute-start(bf16[32,2048]{1,0:T(8,128)(2,1)} %refs_0_.1), channel_id=1, source_target_pairs={{0,8},{2,10},{4,12},{6,14},{8,0},{10,2},{12,4},{14,6},{16,24},{18,... | collective-permute-start | bytes 393224 | tf_op jit(solution)/shard_map/ppermute | solution.py:135
  13.9 9.6 %collective-permute-start.8 = (bf16[32,2048]{1,0:T(8,128)(2,1)}, bf16[32,2048]{1,0:T(8,128)(2,1)S(1)}, u32[]{:S(2)}, u32[]{:S(2)}) collective-permute-start(bf16[32,2048]{1,0:T(8,128)(2,1)} %refs_0_.1), channel_id=1, source_target_pairs={{0,24},{2,26},{4,28},{6,30},{8,16},{10,18},{12,20},{14,22},{16,8},... | collective-permute-start | bytes 393224 | tf_op jit(solution)/shard_map/ppermute | solution.py:135
  13.9 1.0 %copy-start.1 = (bf16[64,2048]{1,0:T(8,128)(2,1)S(1)}, bf16[64,2048]{1,0:T(8,128)(2,1)}, u32[]{:S(2)}) copy-start(bf16[64,2048]{1,0:T(8,128)(2,1)} %refs_1_.1) | copy-start | bytes 786436
  14.9 0.9 %copy-start.2 = (bf16[32,2048]{1,0:T(8,128)(2,1)S(1)}, bf16[32,2048]{1,0:T(8,128)(2,1)}, u32[]{:S(2)}) copy-start(bf16[32,2048]{1,0:T(8,128)(2,1)} %refs_0_.1) | copy-start | bytes 393220
  15.8 0.7 %copy-start.3 = (bf16[32,2048]{1,0:T(8,128)(2,1)}, bf16[32,2048]{1,0:T(8,128)(2,1)S(1)}, u32[]{:S(2)}) copy-start(bf16[32,2048]{1,0:T(8,128)(2,1)S(1)} %get-tuple-element.24.refs_0_) | copy-start | bytes 393220
  19.8 0.9 %copy-start.4 = (bf16[32,2048]{1,0:T(8,128)(2,1)S(1)}, bf16[32,2048]{1,0:T(8,128)(2,1)}, u32[]{:S(2)}) copy-start(bf16[32,2048]{1,0:T(8,128)(2,1)} %copy-done.3) | copy-start | bytes 393220
  20.7 37.0 %copy-start.6 = (f32[256]{0:T(256)S(1)}, f32[256]{0:T(256)}, u32[]{:S(2)}) copy-start(f32[256]{0:T(256)} %param.10) | copy-start | bytes 3076
  20.7 42.2 %copy-start = (bf16[1024,1024]{1,0:T(8,128)(2,1)S(1)}, bf16[1024,1024]{1,0:T(8,128)(2,1)}, u32[]{:S(2)}) copy-start(bf16[1024,1024]{1,0:T(8,128)(2,1)} %refs_12_.1) | copy-start | bytes 6291460
  20.7 42.2 %copy-start.5 = (f32[1024]{0:T(1024)S(1)}, f32[1024]{0:T(1024)}, u32[]{:S(2)}) copy-start(f32[1024]{0:T(1024)} %param.11) | copy-start | bytes 12292
  24.6 4.3 %collective-permute-start.9 = (bf16[4,32,256]{2,1,0:T(8,128)(2,1)S(1)}, bf16[4,32,256]{2,1,0:T(8,128)(2,1)S(1)}, u32[]{:S(2)}, u32[]{:S(2)}) collective-permute-start(bf16[4,32,256]{2,1,0:T(8,128)(2,1)S(1)} %get-tuple-element.30), channel_id=1, source_target_pairs={{0,1},{1,0},{2,3},{3,2},{4,5},{5,4},{6,7},{7,6},{8,9},{9,8},{10,11... | collective-permute-start | bytes 196616 | tf_op jit(solution)/shard_map/ppermute | solution.py:135
  26.1 4.5 %collective-permute-start.10 = (f32[4,32,256]{2,1,0:T(8,128)S(1)}, f32[4,32,256]{2,1,0:T(8,128)S(1)}, u32[]{:S(2)}, u32[]{:S(2)}) collective-permute-start(f32[4,32,256]{2,1,0:T(8,128)S(1)} %get-tuple-element.29.refs_4_.refs_0_), channel_id=1, source_target_pairs={{0,2},{2,0},{4,6},{6,4},{8,10},{10,8},{12,14},{14,12},{16,18},{18,... | collective-permute-start | bytes 393224 | tf_op jit(solution)/shard_map/ppermute | solution.py:135
  26.1 4.5 %collective-permute-start.4 = (bf16[4,32,256]{2,1,0:T(8,128)(2,1)S(1)}, bf16[4,32,256]{2,1,0:T(8,128)(2,1)S(1)}, u32[]{:S(2)}, u32[]{:S(2)}) collective-permute-start(bf16[4,32,256]{2,1,0:T(8,128)(2,1)S(1)} %get-tuple-element.27), channel_id=1, source_target_pairs={{0,1},{1,0},{2,3},{3,2},{4,5},{5,4},{6,7},{7,6},{8,9},{9,8},{10,11... | collective-permute-start | bytes 196616 | tf_op jit(solution)/shard_map/ppermute | solution.py:135
  26.7 14.0 %collective-permute-start.5 = (f32[4,32,256]{2,1,0:T(8,128)S(1)}, f32[4,32,256]{2,1,0:T(8,128)S(1)}, u32[]{:S(2)}, u32[]{:S(2)}) collective-permute-start(f32[4,32,256]{2,1,0:T(8,128)S(1)} %get-tuple-element.26.refs_0_), channel_id=1, source_target_pairs={{0,2},{2,0},{4,6},{6,4},{8,10},{10,8},{12,14},{14,12},{16,18},{18,... | collective-permute-start | bytes 393224 | tf_op jit(solution)/shard_map/ppermute | solution.py:135
  28.9 1.7 %collective-permute-start.11 = (bf16[4,32,256]{2,1,0:T(8,128)(2,1)S(1)}, bf16[4,32,256]{2,1,0:T(8,128)(2,1)S(1)}, u32[]{:S(2)}, u32[]{:S(2)}) collective-permute-start(bf16[4,32,256]{2,1,0:T(8,128)(2,1)S(1)} %collective-permute-done.9.refs_5_.refs_1_), channel_id=1, source_target_pairs={{0,2},{2,0},{4,6},{6,4},{8,10},{10,8},{12,14},{14,12},{16,18},{18,... | collective-permute-start | bytes 196616 | tf_op jit(solution)/shard_map/ppermute | solution.py:135
  30.6 7.4 %collective-permute-start.6 = (bf16[4,32,256]{2,1,0:T(8,128)(2,1)S(1)}, bf16[4,32,256]{2,1,0:T(8,128)(2,1)S(1)}, u32[]{:S(2)}, u32[]{:S(2)}) collective-permute-start(bf16[4,32,256]{2,1,0:T(8,128)(2,1)S(1)} %collective-permute-done.4.refs_1_), channel_id=1, source_target_pairs={{0,2},{2,0},{4,6},{6,4},{8,10},{10,8},{12,14},{14,12},{16,18},{18,... | collective-permute-start | bytes 196616 | tf_op jit(solution)/shard_map/ppermute | solution.py:135
  31.6 13.6 %collective-permute-start.19 = (bf16[2,64,256]{2,1,0:T(8,128)(2,1)S(1)}, bf16[2,64,256]{2,1,0:T(8,128)(2,1)S(1)}, u32[]{:S(2)}, u32[]{:S(2)}) collective-permute-start(bf16[2,64,256]{2,1,0:T(8,128)(2,1)S(1)} %get-tuple-element.39), channel_id=1, source_target_pairs={{0,16},{2,18},{4,20},{6,22},{8,24},{10,26},{12,28},{14,30},{16,0},... | collective-permute-start | bytes 196616 | tf_op jit(solution)/shard_map/ppermute | solution.py:135
  35.9 12.3 %collective-permute-start.20 = (bf16[2,64,256]{2,1,0:T(8,128)(2,1)S(1)}, bf16[2,64,256]{2,1,0:T(8,128)(2,1)S(1)}, u32[]{:S(2)}, u32[]{:S(2)}) collective-permute-start(bf16[2,64,256]{2,1,0:T(8,128)(2,1)S(1)} %get-tuple-element.40), channel_id=1, source_target_pairs={{0,20},{2,22},{4,16},{6,18},{8,28},{10,30},{12,24},{14,26},{16,4},... | collective-permute-start | bytes 196616 | tf_op jit(solution)/shard_map/ppermute | solution.py:135
  36.9 11.8 %collective-permute-start.21 = (bf16[2,64,256]{2,1,0:T(8,128)(2,1)S(1)}, bf16[2,64,256]{2,1,0:T(8,128)(2,1)S(1)}, u32[]{:S(2)}, u32[]{:S(2)}) collective-permute-start(bf16[2,64,256]{2,1,0:T(8,128)(2,1)S(1)} %get-tuple-element.41), channel_id=1, source_target_pairs={{0,24},{2,26},{4,28},{6,30},{8,16},{10,18},{12,20},{14,22},{16,8},... | collective-permute-start | bytes 196616 | tf_op jit(solution)/shard_map/ppermute | solution.py:135
  38.0 11.2 %collective-permute-start.22 = (bf16[2,64,256]{2,1,0:T(8,128)(2,1)S(1)}, bf16[2,64,256]{2,1,0:T(8,128)(2,1)S(1)}, u32[]{:S(2)}, u32[]{:S(2)}) collective-permute-start(bf16[2,64,256]{2,1,0:T(8,128)(2,1)S(1)} %get-tuple-element.42), channel_id=1, source_target_pairs={{0,28},{2,30},{4,24},{6,26},{8,20},{10,22},{12,16},{14,18},{16,12}... | collective-permute-start | bytes 196616 | tf_op jit(solution)/shard_map/ppermute | solution.py:135
  42.1 10.8 %collective-permute-start.15 = (bf16[2,64,256]{2,1,0:T(8,128)(2,1)S(1)}, bf16[2,64,256]{2,1,0:T(8,128)(2,1)S(1)}, u32[]{:S(2)}, u32[]{:S(2)}) collective-permute-start(bf16[2,64,256]{2,1,0:T(8,128)(2,1)S(1)} %get-tuple-element.35), channel_id=1, source_target_pairs={{0,16},{2,18},{4,20},{6,22},{8,24},{10,26},{12,28},{14,30},{16,0},... | collective-permute-start | bytes 196616 | tf_op jit(solution)/shard_map/ppermute | solution.py:135
  45.1 10.2 %collective-permute-start.16 = (bf16[2,64,256]{2,1,0:T(8,128)(2,1)S(1)}, bf16[2,64,256]{2,1,0:T(8,128)(2,1)S(1)}, u32[]{:S(2)}, u32[]{:S(2)}) collective-permute-start(bf16[2,64,256]{2,1,0:T(8,128)(2,1)S(1)} %get-tuple-element.36), channel_id=1, source_target_pairs={{0,20},{2,22},{4,16},{6,18},{8,28},{10,30},{12,24},{14,26},{16,4},... | collective-permute-start | bytes 196616 | tf_op jit(solution)/shard_map/ppermute | solution.py:135
  48.2 14.4 %collective-permute-start.12 = (bf16[2,128,256]{2,1,0:T(8,128)(2,1)}, bf16[2,128,256]{2,1,0:T(8,128)(2,1)S(1)}, u32[]{:S(2)}, u32[]{:S(2)}) collective-permute-start(bf16[2,128,256]{2,1,0:T(8,128)(2,1)} %get-tuple-element.32), channel_id=1, source_target_pairs={{0,4},{2,6},{4,0},{6,2},{8,12},{10,14},{12,8},{14,10},{16,20},{18,... | collective-permute-start | bytes 393224 | tf_op jit(solution)/shard_map/ppermute | solution.py:135
  48.7 13.9 %collective-permute-start.13 = (bf16[2,128,256]{2,1,0:T(8,128)(2,1)S(1)}, bf16[2,128,256]{2,1,0:T(8,128)(2,1)S(1)}, u32[]{:S(2)}, u32[]{:S(2)}) collective-permute-start(bf16[2,128,256]{2,1,0:T(8,128)(2,1)S(1)} %get-tuple-element.33), channel_id=1, source_target_pairs={{0,8},{2,10},{4,12},{6,14},{8,0},{10,2},{12,4},{14,6},{16,24},{18,... | collective-permute-start | bytes 393224 | tf_op jit(solution)/shard_map/ppermute | solution.py:135
  49.2 13.7 %collective-permute-start.14 = (bf16[2,128,256]{2,1,0:T(8,128)(2,1)S(1)}, bf16[2,128,256]{2,1,0:T(8,128)(2,1)S(1)}, u32[]{:S(2)}, u32[]{:S(2)}) collective-permute-start(bf16[2,128,256]{2,1,0:T(8,128)(2,1)S(1)} %get-tuple-element.34), channel_id=1, source_target_pairs={{0,12},{2,14},{4,8},{6,10},{8,4},{10,6},{12,0},{14,2},{16,28},{18,... | collective-permute-start | bytes 393224 | tf_op jit(solution)/shard_map/ppermute | solution.py:135
  53.0 6.3 %collective-permute-start.17 = (bf16[2,64,256]{2,1,0:T(8,128)(2,1)}, bf16[2,64,256]{2,1,0:T(8,128)(2,1)S(1)}, u32[]{:S(2)}, u32[]{:S(2)}) collective-permute-start(bf16[2,64,256]{2,1,0:T(8,128)(2,1)} %get-tuple-element.37), channel_id=1, source_target_pairs={{0,24},{2,26},{4,28},{6,30},{8,16},{10,18},{12,20},{14,22},{16,8},... | collective-permute-start | bytes 196616 | tf_op jit(solution)/shard_map/ppermute | solution.py:135
  55.3 7.3 %collective-permute-start.18 = (bf16[2,64,256]{2,1,0:T(8,128)(2,1)}, bf16[2,64,256]{2,1,0:T(8,128)(2,1)S(1)}, u32[]{:S(2)}, u32[]{:S(2)}) collective-permute-start(bf16[2,64,256]{2,1,0:T(8,128)(2,1)} %get-tuple-element.38), channel_id=1, source_target_pairs={{0,28},{2,30},{4,24},{6,26},{8,20},{10,22},{12,16},{14,18},{16,12}... | collective-permute-start | bytes 196616 | tf_op jit(solution)/shard_map/ppermute | solution.py:135
